TPU v7x, 32 devices: a whole 2x2x4 slice. The times are simulated.
32 devices in a mesh: fsdp: 16 (over z, y, x), tensor: 2 (over core).
Axes of the slice: x: 2, y: 2, z: 4, core: 2. Of those that a mesh axis runs over, the one named last changes fastest.
Arguments:
- tokens: bfloat16 [64, 577, 1024], P(('fsdp', 'tensor')), may hold values from -6 to 6
- cotangent: bfloat16 [64, 577, 1024], P(('fsdp', 'tensor')), may hold values from -6 to 6
- adapter_index: int32 [64], P('fsdp'), may hold values from 0 to 7
- filled: int32 [64], P('fsdp'), may hold values 0 or 1
- ln1_gain: bfloat16 [1024], replicated, may hold values from 0.5 to 1.5
- ln1_shift: bfloat16 [1024], replicated, may hold values from -2 to 2
- qkv_weight: bfloat16 [1024, 3, 1024], P('fsdp', None, 'tensor'), may hold values from -0.1875 to 0.1875
- qv_bias: bfloat16 [2, 1024], replicated, may hold values from -3 to 3
- out_weight: bfloat16 [1024, 1024], P('tensor', 'fsdp'), may hold values from -0.75 to 0.75
- out_bias: bfloat16 [1024], replicated, may hold values from -3 to 3
- ln2_gain: bfloat16 [1024], replicated, may hold values from 0.5 to 1.5
- ln2_shift: bfloat16 [1024], replicated, may hold values from -2 to 2
- fc1_weight: bfloat16 [1024, 4096], P('fsdp', 'tensor'), may hold values from -0.1875 to 0.1875
- fc1_bias: bfloat16 [4096], replicated, may hold values from -3 to 3
- fc2_weight: bfloat16 [4096, 1024], P('tensor', 'fsdp'), may hold values from -0.09375 to 0.09375
- fc2_bias: bfloat16 [1024], replicated, may hold values from -3 to 3
- qkv_down: bfloat16 [8, 16, 1024], P(None, None, ('fsdp', 'tensor')), may hold values from -0.1875 to 0.1875
- qkv_up: bfloat16 [8, 16, 3072], P(None, None, ('fsdp', 'tensor')), may hold values from -0.75 to 0.75
- out_down: bfloat16 [8, 16, 1024], P(None, None, ('fsdp', 'tensor')), may hold values from -0.75 to 0.75
- out_up: bfloat16 [8, 16, 1024], P(None, None, ('fsdp', 'tensor')), may hold values from -0.75 to 0.75
- fc1_down: bfloat16 [8, 16, 1024], P(None, None, ('fsdp', 'tensor')), may hold values from -0.1875 to 0.1875
- fc1_up: bfloat16 [8, 16, 4096], P(None, None, ('fsdp', 'tensor')), may hold values from -0.75 to 0.75
- fc2_down: bfloat16 [8, 16, 4096], P(None, None, ('fsdp', 'tensor')), may hold values from -0.1875 to 0.1875
- fc2_up: bfloat16 [8, 16, 1024], P(None, None, ('fsdp', 'tensor')), may hold values from -0.75 to 0.75
Outputs:
- outputs: bfloat16 [64, 577, 1024], P(('fsdp', 'tensor'))
- input_grad: float32 [64, 577, 1024], P(('fsdp', 'tensor'))
- grad_qkv_down: float32 [8, 16, 1024], P(None, None, ('fsdp', 'tensor'))
- grad_qkv_up: float32 [8, 16, 3072], P(None, None, ('fsdp', 'tensor'))
- grad_out_down: float32 [8, 16, 1024], P(None, None, ('fsdp', 'tensor'))
- grad_out_up: float32 [8, 16, 1024], P(None, None, ('fsdp', 'tensor'))
- grad_fc1_down: float32 [8, 16, 1024], P(None, None, ('fsdp', 'tensor'))
- grad_fc1_up: float32 [8, 16, 4096], P(None, None, ('fsdp', 'tensor'))
- grad_fc2_down: float32 [8, 16, 4096], P(None, None, ('fsdp', 'tensor'))
- grad_fc2_up: float32 [8, 16, 1024], P(None, None, ('fsdp', 'tensor'))
All inputs are finite; a program needn't handle non-finite values. No bound on the sum of `filled` on one device may be relied on, other than what follows from the above.
Results may differ from a plain program's by a relative error of at most 0.014.
Values may be sent and summed in bfloat16 or wider, within the bound.
No kernel may reach another device: no remote copies, remote signals or barrier semaphores. Data moves between devices by JAX's collectives and lax.ppermute only.
A program may use at most 256 MiB of HBM per device.

v0:
```python
import math
from functools import partial

import jax
import jax.numpy as jnp
from jax import lax
from jax.experimental import pallas as pl
from jax.experimental.pallas import tpu as pltpu
from jax.sharding import PartitionSpec as P

D = 1024
HEADS = 16
HEAD_DIM = 64
FF = 4096
SEQ = 577
RANK = 16
ADAPTERS = 8
STACK = ADAPTERS * RANK
TILE = 1024
STACK_SHAPES = ((16, 2, 32, STACK), (16, 2, 96, STACK))

epsilon = 1e-05
bf16 = jnp.bfloat16
f32 = jnp.float32
NN = (((1,), (0,)), ((), ()))
NT = (((1,), (1,)), ((), ()))
TN = (((0,), (0,)), ((), ()))
BOTH = ("fsdp", "tensor")


def dot(left, right, dims):
    return lax.dot_general(left, right, dims, preferred_element_type=f32)


def params():
    return pltpu.CompilerParams(vmem_limit_bytes=60 << 20)


def cost(flops, moved, exps=0):
    return pl.CostEstimate(flops=flops, bytes_accessed=moved, transcendentals=exps)


def smem():
    return pl.BlockSpec(memory_space=pltpu.SMEM)


def whole(shape):
    return pl.BlockSpec(shape, lambda *_: (0,) * len(shape), pipeline_mode=pl.Buffered(1))


GAIN1, SHIFT1, OUT_BIAS, GAIN2, SHIFT2, BIAS2, BIAS1 = range(7)


def vector(place):
    return pl.BlockSpec((1, D), lambda *_: (0, place), pipeline_mode=pl.Buffered(1))


def image_rows(width=D):
    return pl.BlockSpec((pl.Squeezed(), SEQ, width), lambda i: (i, 0, 0))


def normalize(values):
    center = values - jnp.mean(values, axis=-1, keepdims=True)
    inverse = lax.rsqrt(jnp.mean(center * center, axis=-1, keepdims=True) + epsilon)
    return center * inverse, inverse


def norm_back(upstream, normed, inverse, gain_row):
    scaled = upstream * gain_row
    return inverse * (
        scaled
        - jnp.mean(scaled, axis=-1, keepdims=True)
        - normed * jnp.mean(scaled * normed, axis=-1, keepdims=True)
    )


def chosen_lanes(adapter):
    lanes = lax.broadcasted_iota(jnp.int32, (1, STACK), 1)
    return (lanes // RANK) == adapter


def keep(product, adapter):
    return jnp.where(chosen_lanes(adapter), product, 0.0).astype(bf16)


def add_to(ref, value, first):
    @pl.when(first)
    def _():
        ref[...] = value

    @pl.when(jnp.logical_not(first))
    def _():
        ref[...] += value


def flat(block):
    return block.reshape(D, block.shape[-1])


def any_space():
    return pl.BlockSpec(memory_space=pl.ANY)


def untangle_kernel(mixed_ref, out_ref):
    for image in range(out_ref.shape[0]):
        out_ref[image] = mixed_ref[:, image, :]


def untangle(array):
    images = array.shape[0]
    return pl.pallas_call(
        untangle_kernel,
        grid=(1,),
        in_specs=[whole((SEQ, images, D))],
        out_specs=whole((images, SEQ, D)),
        out_shape=jax.ShapeDtypeStruct((images, SEQ, D), array.dtype),
        compiler_params=pltpu.CompilerParams(vmem_limit_bytes=32 << 20),
        name="untangle",
    )(array.transpose(1, 0, 2))


class Stream:
    def __init__(self, sources, lane, width, slots, sems):
        self.sources, self.lane, self.width = sources, lane, width
        self.slots, self.sems = slots, sems

    def copy(self, source, inner, slot):
        lanes = pl.ds(self.lane, self.width)
        return pltpu.make_async_copy(
            source.at[inner, :, :, lanes], self.slots.at[slot], self.sems.at[slot]
        )

    def start(self, group, slot):
        offset = 0
        for source in self.sources:
            count = source.shape[0]

            @pl.when(jnp.logical_and(group >= offset, group < offset + count))
            def _(source=source, offset=offset):
                self.copy(source, group - offset, slot).start()

            offset += count

    def wait(self, slot):
        self.copy(self.sources[0], 0, slot).wait()


def spread_copies(sources, lane, parts, table_ref, weight_ref, sem):
    members, rows, total = weight_ref.shape
    groups = group_count(sources)
    width = total // parts // groups
    group = 0
    for source in sources:
        for inner in range(source.shape[0]):
            start = pl.multiple_of(table_ref[group] * width, width)
            for part in range(parts):
                yield pltpu.make_async_copy(
                    source.at[inner, :, :, pl.ds(lane + part * width, width)],
                    weight_ref.at[:, :, pl.ds(part * width * groups + start, width)],
                    sem.at[group * parts + part],
                )
            group += 1


def spread_scratch(sources, parts):
    members, rows = sources[0].shape[1:3]
    return [
        pltpu.VMEM((members, rows, parts * D), bf16),
        pltpu.SemaphoreType.DMA((group_count(sources) * parts,)),
    ]


def qkv_kernel(count, moves, *refs):
    table_ref, places_ref, index_ref, tokens_ref = refs[:4]
    sources = refs[4 : 4 + count]
    stacks = refs[4 + count : 6 + count]
    bias_ref, gain_ref, shift_ref = refs[6 + count : 9 + count]
    (
        q_ref, k_ref, v_ref, low_ref, down_ref, up_ref,
        a_s, low_s, up_s, slots, sems, stack_sems,
    ) = refs[9 + count :]
    copies = [
        pltpu.make_async_copy(
            source(stacks[part], places_ref),
            target((down_ref, up_ref)[out], places_ref),
            stack_sems.at[number],
        )
        for number, (part, out, source, target) in enumerate(moves)
    ]
    group = pl.program_id(0)
    image = pl.program_id(1)
    width = q_ref.shape[-1]
    stream = Stream(sources, 0, 3 * width, slots, sems)
    slot = group % 2

    @pl.when(jnp.logical_and(group == 0, image == 0))
    def _():
        for copy in copies:
            copy.start()
        stream.start(group, 0)

    @pl.when(group == 0)
    def _():
        normed, _ = normalize(tokens_ref[...].astype(f32))
        a_s[image] = (normed * gain_ref[...] + shift_ref[...]).astype(bf16)

    @pl.when(jnp.logical_and(group == 0, image == 0))
    def _():
        for copy in copies:
            copy.wait()
        up_s[...] = up_ref[...].reshape(3 * D, STACK)

    @pl.when(group == 0)
    def _():
        down = down_ref[...].reshape(D, STACK)
        low_s[image] = keep(dot(a_s[image], down, NN), index_ref[0, image])

    @pl.when(image == 0)
    def _():
        stream.wait(slot)

        @pl.when(group + 1 < pl.num_programs(0))
        def _():
            stream.start(group + 1, 1 - slot)

    a = a_s[image]
    low = low_s[image]
    low_ref[...] = low
    weight = flat(slots[slot])
    start = pl.multiple_of(table_ref[group] * width, width)
    bias = bias_ref[...].astype(f32)
    for part, out_ref in enumerate((q_ref, k_ref, v_ref)):
        value = dot(a, weight[:, part * width : (part + 1) * width], NN)
        value += dot(low, up_s[pl.ds(part * D + start, width), :], NT)
        if part != 1:
            value += bias[part // 2 : part // 2 + 1]
        out_ref[...] = value.astype(bf16)


def group_count(sources):
    return sum(source.shape[0] for source in sources)


def qkv_project(tokens, sources, table, places, stacks, moves, who, bias, vectors):
    images = tokens.shape[0]
    members, rows = sources[0].shape[1:3]
    groups = group_count(sources)
    width = D // groups
    sq = pl.Squeezed()
    out = pl.BlockSpec((sq, SEQ, width), lambda g, i, t: (i, 0, t[g]))
    grid_spec = pltpu.PrefetchScalarGridSpec(
        num_scalar_prefetch=1,
        grid=(groups, images),
        in_specs=[smem(), smem(), pl.BlockSpec((sq, SEQ, D), lambda g, i, t: (i, 0, 0))]
        + [any_space()] * (len(sources) + 2)
        + [pl.BlockSpec((2, width), lambda g, i, t: (0, t[g])), vector(GAIN1), vector(SHIFT1)],
        out_specs=[out, out, out, pl.BlockSpec((sq, SEQ, STACK), lambda g, i, t: (i, 0, 0))]
        + [pl.BlockSpec(shape, lambda g, i, t: (0, 0, 0, 0)) for shape in STACK_SHAPES],
        scratch_shapes=[
            pltpu.VMEM((images, SEQ, D), bf16),
            pltpu.VMEM((images, SEQ, STACK), bf16),
            pltpu.VMEM((3 * D, STACK), bf16),
            pltpu.VMEM((2, members, rows, 3 * width), bf16),
            pltpu.SemaphoreType.DMA((2,)),
            pltpu.SemaphoreType.DMA((len(moves),)),
        ],
    )
    return pl.pallas_call(
        partial(qkv_kernel, len(sources), moves),
        grid_spec=grid_spec,
        out_shape=[jax.ShapeDtypeStruct((images, SEQ, D), bf16)] * 3
        + [jax.ShapeDtypeStruct((images, SEQ, STACK), bf16)]
        + [jax.ShapeDtypeStruct(shape, bf16) for shape in STACK_SHAPES],
        compiler_params=params(),
        cost_estimate=cost(6 * images * SEQ * D * D, 20 << 20),
        name="qkv_project",
    )(table, places, who, tokens, *sources, *stacks, bias, vectors, vectors)


def attend_kernel(q_ref, k_ref, v_ref, o_ref, w_ref, scale_ref):
    q = q_ref[...]
    k = k_ref[...]
    v = v_ref[...]
    low = lax.broadcasted_iota(jnp.int32, q.shape, 1) < HEAD_DIM
    both = jnp.concatenate([v, jnp.ones_like(v)], axis=1)
    outs = []
    for head in range(2):
        own = low if head == 0 else jnp.logical_not(low)
        queries = jnp.where(own, q * HEAD_DIM**-0.5, jnp.zeros_like(q)).astype(bf16)
        scores = dot(queries, k, NT)
        raised = jnp.exp(scores - jnp.max(scores, axis=-1, keepdims=True)).astype(bf16)
        w_ref[head] = raised
        outs.append(dot(raised, both, NN))
    width = v.shape[-1]
    scale = 1.0 / jnp.where(low, outs[0][:, width:], outs[1][:, width:])
    scale_ref[...] = scale
    o_ref[...] = (jnp.where(low, outs[0][:, :width], outs[1][:, :width]) * scale).astype(bf16)


def pair_rows(image):
    return pl.BlockSpec((pl.Squeezed(), SEQ, 2 * HEAD_DIM), lambda h: (image, 0, h))


def pair_weights(image):
    return pl.BlockSpec((2, SEQ, SEQ), lambda h: (image * (HEADS // 2) + h, 0, 0))


def into(kernel, inputs):
    def body(*refs):
        kernel(*refs[:inputs], *refs[len(refs) - (len(refs) - inputs) // 2 :])

    return body


def per_image(kernel, name, image, inputs, in_specs, outs, out_specs, filled, flops, moved, exps):
    count = len(inputs)
    if filled is None:
        return pl.pallas_call(
            kernel, grid=(HEADS // 2,), in_specs=in_specs, out_specs=out_specs, out_shape=outs,
            compiler_params=params(), cost_estimate=cost(flops, moved, exps), name=name,
        )(*inputs)
    return pl.pallas_call(
        into(kernel, count), grid=(HEADS // 2,), in_specs=in_specs + [any_space()] * len(outs),
        out_specs=out_specs, out_shape=outs,
        input_output_aliases={count + n: n for n in range(len(outs))},
        compiler_params=params(), cost_estimate=cost(flops, moved, exps), name=name,
    )(*inputs, *filled)


def attend(q, k, v, image, filled):
    images = q.shape[0]
    outs = [
        jax.ShapeDtypeStruct((images, SEQ, D), bf16),
        jax.ShapeDtypeStruct((images * HEADS, SEQ, SEQ), bf16),
        jax.ShapeDtypeStruct((images, SEQ, D), f32),
    ]
    return per_image(
        attend_kernel, "attend", image, (q, k, v), [pair_rows(image)] * 3, outs,
        [pair_rows(image), pair_weights(image), pair_rows(image)], filled,
        16 * SEQ * SEQ * D, 20 << 20, HEADS * SEQ * SEQ,
    )


def attend_back_kernel(
    q_ref, k_ref, v_ref, do_ref, o_ref, w_ref, scale_ref, dq_ref, dk_ref, dv_ref
):
    q = q_ref[...]
    k = k_ref[...]
    v = v_ref[...]
    do = (do_ref[...].astype(f32) * scale_ref[...]).astype(bf16)
    products = do.astype(f32) * o_ref[...].astype(f32)
    low = lax.broadcasted_iota(jnp.int32, q.shape, 1) < HEAD_DIM
    grads = []
    for head in range(2):
        own = low if head == 0 else jnp.logical_not(low)
        mixed_grad = jnp.where(own, do, jnp.zeros_like(do))
        inner = jnp.sum(jnp.where(own, products, 0.0), axis=-1, keepdims=True)
        raised = w_ref[head]
        prob_grad = dot(mixed_grad, v, NT)
        score_grad = (raised.astype(f32) * (prob_grad - inner)).astype(bf16)
        grads.append((dot(score_grad, k, NN), dot(score_grad, q, TN), dot(raised, do, TN)))
    scale = HEAD_DIM**-0.5
    dq_ref[...] = (jnp.where(low, grads[0][0], grads[1][0]) * scale).astype(bf16)
    dk_ref[...] = (jnp.where(low, grads[0][1], grads[1][1]) * scale).astype(bf16)
    dv_ref[...] = jnp.where(low, grads[0][2], grads[1][2]).astype(bf16)


def attend_back(q, k, v, do, o, kept, image, filled):
    outs = [jax.ShapeDtypeStruct(q.shape, bf16)] * 3
    return per_image(
        attend_back_kernel, "attend_back", image, (q, k, v, do, o, *kept),
        [pair_rows(image)] * 5 + [pair_weights(image), pair_rows(image)], outs,
        [pair_rows(image)] * 3, filled, 32 * SEQ * SEQ * D, 24 << 20, 0,
    )


def out_kernel(count, lane, *refs):
    table_ref, index_ref, filled_ref, tokens_ref, o_ref = refs[:5]
    sources = refs[5 : 5 + count]
    down_ref, up_ref, bias_ref, h_ref, low_ref, weight_s, sems = refs[5 + count :]
    image = pl.program_id(0)

    @pl.when(image == 0)
    def _():
        for copy in spread_copies(sources, lane, 1, table_ref, weight_s, sems):
            copy.start()

    low = keep(dot(o_ref[...], down_ref[...], NN), index_ref[0, image])
    low_ref[...] = low

    @pl.when(image == 0)
    def _():
        for copy in spread_copies(sources, lane, 1, table_ref, weight_s, sems):
            copy.wait()

    value = dot(o_ref[...], flat(weight_s[...]), NT) + dot(low, up_ref[...], NT) + bias_ref[...]
    h_ref[...] = tokens_ref[...].astype(f32) + filled_ref[1, image].astype(f32) * value


def out_project(tokens, o, sources, lane, table, down, up, who, vectors):
    images = tokens.shape[0]
    return pl.pallas_call(
        partial(out_kernel, len(sources), lane),
        grid=(images,),
        in_specs=[smem(), smem(), smem(), image_rows(), image_rows()]
        + [any_space()] * len(sources)
        + [whole((D, STACK)), whole((D, STACK)), vector(OUT_BIAS)],
        out_specs=[image_rows(), image_rows(STACK)],
        out_shape=[
            jax.ShapeDtypeStruct((images, SEQ, D), f32),
            jax.ShapeDtypeStruct((images, SEQ, STACK), bf16),
        ],
        scratch_shapes=spread_scratch(sources, 1),
        compiler_params=params(),
        cost_estimate=cost(2 * images * SEQ * D * D, 12 << 20),
        name="out_project",
    )(table, who, who, tokens, o, *sources, down, up, vectors)


def out_back_kernel(count, lane, *refs):
    table_ref, index_ref, filled_ref, dh_ref, o_ref, low_ref = refs[:6]
    sources = refs[6 : 6 + count]
    down_ref, up_ref, do_ref, grad_up_ref, grad_down_ref = refs[6 + count : 11 + count]
    grad_up_s, grad_down_s, weight_s, sems = refs[11 + count :]
    image = pl.program_id(0)
    last = image == pl.num_programs(0) - 1

    @pl.when(image == 0)
    def _():
        for copy in spread_copies(sources, lane, 1, table_ref, weight_s, sems):
            copy.start()
        grad_up_s[...] = jnp.zeros_like(grad_up_s)
        grad_down_s[...] = jnp.zeros_like(grad_down_s)

    branch = (dh_ref[...] * filled_ref[1, image].astype(f32)).astype(bf16)
    low_grad = keep(dot(branch, up_ref[...], NN), index_ref[0, image])
    grad_up_s[...] += dot(low_ref[...], branch, TN)
    grad_down_s[...] += dot(low_grad, o_ref[...], TN)

    @pl.when(image == 0)
    def _():
        for copy in spread_copies(sources, lane, 1, table_ref, weight_s, sems):
            copy.wait()

    value = dot(branch, flat(weight_s[...]), NN) + dot(low_grad, down_ref[...], NT)
    do_ref[...] = value.astype(bf16)

    @pl.when(last)
    def _():
        grad_up_ref[...] = grad_up_s[...].T.astype(bf16)
        grad_down_ref[...] = grad_down_s[...].T.astype(bf16)


def out_back(dh, o, low, sources, lane, table, down, up, who):
    images = dh.shape[0]
    grad = pl.BlockSpec((D, STACK), lambda i: (0, 0))
    return pl.pallas_call(
        partial(out_back_kernel, len(sources), lane),
        grid=(images,),
        in_specs=[smem(), smem(), smem(), image_rows(), image_rows(), image_rows(STACK)]
        + [any_space()] * len(sources)
        + [whole((D, STACK)), whole((D, STACK))],
        out_specs=[image_rows(), grad, grad],
        out_shape=[jax.ShapeDtypeStruct((images, SEQ, D), bf16)]
        + [jax.ShapeDtypeStruct((D, STACK), bf16)] * 2,
        scratch_shapes=[pltpu.VMEM((STACK, D), f32)] * 2 + spread_scratch(sources, 1),
        compiler_params=params(),
        cost_estimate=cost(2 * images * SEQ * D * D, 12 << 20),
        name="out_back",
    )(table, who, who, dh, o, low, *sources, down, up)


def mlp_kernel(sides, *refs):
    index_ref, filled_ref, h_ref, cot_ref, first_ref, second_ref, down1_ref = refs[:7]
    up1_refs = refs[7 : 7 + sides]
    down2_refs = refs[7 + sides : 7 + 2 * sides]
    (
        up2_ref, bias1_ref, bias2_ref, gain_ref, shift_ref,
        out_ref, dh_ref, grad_up2_ref, grad_down2_ref, grad_up1_ref, grad_down1_ref,
        a_s, dz_s, low3_s, dlow4_s, z_s, da_s, low4_s, dlow3_s,
        grad_up2_s, grad_down2_s, grad_up1_s, grad_down1_s,
    ) = refs[7 + 2 * sides :]
    width = grad_up1_ref.shape[0]
    tall = lambda parts: jnp.concatenate([part[...] for part in parts], axis=2).reshape(
        width, STACK
    )
    up1 = tall(up1_refs)
    down2 = tall(down2_refs)
    tile = pl.program_id(0)
    image = pl.program_id(1)
    last = tile == pl.num_programs(0) - 1
    final = image == pl.num_programs(1) - 1
    adapter = index_ref[0, image]
    mask = filled_ref[1, image].astype(f32)

    @pl.when(image == 0)
    def _():
        grad_down2_s[...] = jnp.zeros_like(grad_down2_s)
        grad_up1_s[...] = jnp.zeros_like(grad_up1_s)

    @pl.when(tile == 0)
    def _():
        for ref in (z_s, da_s, low4_s, dlow3_s):
            ref[image] = jnp.zeros(ref.shape[1:], f32)
        normed, _ = normalize(h_ref[image])
        a = (normed * gain_ref[...] + shift_ref[...]).astype(bf16)
        a_s[image] = a
        dz = (cot_ref[image].astype(f32) * mask).astype(bf16)
        dz_s[image] = dz
        low3_s[image] = keep(dot(a, down1_ref[...], NN), adapter)
        dlow4_s[image] = keep(dot(dz, up2_ref[...], NN), adapter)

    a = a_s[image]
    dz = dz_s[image]
    low3 = low3_s[image]
    dlow4 = dlow4_s[image]
    first = flat(first_ref[...])
    second = flat(second_ref[...])
    before = dot(a, first, NN) + dot(low3, up1, NT) + bias1_ref[...]
    density = jnp.exp(before * before * -0.5) * 0.3989422804014327
    below = 0.5 * lax.erf(before * 0.7071067811865476) + 0.5
    g = (before * below).astype(bf16)
    slope = below + before * density
    dg = dot(dz, second, NN) + dot(dlow4, down2, NT)
    df = (dg * slope).astype(bf16)
    z_s[image] += dot(g, second, NT)
    da_s[image] += dot(df, first, NT)
    low4_s[image] += dot(g, down2, NN)
    dlow3_s[image] += dot(df, up1, NN)
    grad_down2_s[...] += dot(dlow4, g, TN)
    grad_up1_s[...] += dot(low3, df, TN)

    @pl.when(final)
    def _():
        grad_down2_ref[...] = grad_down2_s[...].T.astype(bf16)
        grad_up1_ref[...] = grad_up1_s[...].T.astype(bf16)

    @pl.when(last)
    def _():
        low4 = keep(low4_s[image], adapter)
        h = h_ref[image]
        z = z_s[image] + dot(low4, up2_ref[...], NT) + bias2_ref[...]
        outputs = (h + mask * z).astype(bf16)
        for number in range(out_ref.shape[1]):

            @pl.when(image == number)
            def _(number=number):
                out_ref[:, number, :] = outputs

        add_to(grad_up2_s, dot(low4, dz, TN), image == 0)
        dlow3 = keep(dlow3_s[image], adapter)
        da = da_s[image] + dot(dlow3, down1_ref[...], NT)
        add_to(grad_down1_s, dot(dlow3, a, TN), image == 0)
        normed, inverse = normalize(h)
        dh_ref[...] = cot_ref[image].astype(f32) + norm_back(
            da, normed, inverse, gain_ref[...]
        )

    @pl.when(jnp.logical_and(last, final))
    def _():
        grad_up2_ref[...] = grad_up2_s[...].T.astype(bf16)
        grad_down1_ref[...] = grad_down1_s[...].T.astype(bf16)


def mlp(h, cot, weights, down1, up1, down2, up2, who, vectors):
    images = h.shape[0]
    members, groups, rows, _ = weights.shape
    hidden = FF // groups
    width = min(TILE, hidden)
    per_group = hidden // width
    tiles = FF // width
    sq = pl.Squeezed()

    def weight(base):
        return pl.BlockSpec(
            (members, sq, rows, width),
            lambda j, i: (0, j // per_group, 0, base * per_group + j % per_group),
        )

    tall = pl.BlockSpec((width, STACK), lambda j, i: (j, 0))
    sides = up1 + down2

    def side_block(array, lane):
        shape = (16 * width // FF, 2, FF // 32 // len(up1), STACK)
        return pl.BlockSpec(shape, lambda j, i: (j, 0, 0, lane))

    short = pl.BlockSpec((D, STACK), lambda j, i: (0, 0))
    late = pl.BlockSpec((sq, SEQ, D), lambda j, i: (jnp.where(j == tiles - 1, i, 0), 0, 0))
    return pl.pallas_call(
        partial(mlp_kernel, len(up1)),
        grid=(tiles, images),
        in_specs=[
            smem(),
            smem(),
            whole((images, SEQ, D)),
            whole((images, SEQ, D)),
            weight(0),
            weight(1),
            whole((D, STACK)),
        ]
        + [side_block(*side) for side in sides]
        + [
            whole((D, STACK)),
            pl.BlockSpec((1, width), lambda j, i: (0, BIAS1 * D // width + j)),
            vector(BIAS2),
            vector(GAIN2),
            vector(SHIFT2),
        ],
        out_specs=[pl.BlockSpec((SEQ, images, D), lambda j, i: (0, 0, 0)), late, short, tall, tall, short],
        out_shape=[
            jax.ShapeDtypeStruct((SEQ, images, D), bf16),
            jax.ShapeDtypeStruct((images, SEQ, D), f32),
            jax.ShapeDtypeStruct((D, STACK), bf16),
            jax.ShapeDtypeStruct((FF, STACK), bf16),
            jax.ShapeDtypeStruct((FF, STACK), bf16),
            jax.ShapeDtypeStruct((D, STACK), bf16),
        ],
        scratch_shapes=[
            pltpu.VMEM((images, SEQ, D), bf16),
            pltpu.VMEM((images, SEQ, D), bf16),
            pltpu.VMEM((images, SEQ, STACK), bf16),
            pltpu.VMEM((images, SEQ, STACK), bf16),
            pltpu.VMEM((images, SEQ, D), f32),
            pltpu.VMEM((images, SEQ, D), f32),
            pltpu.VMEM((images, SEQ, STACK), f32),
            pltpu.VMEM((images, SEQ, STACK), f32),
            pltpu.VMEM((STACK, D), f32),
            pltpu.VMEM((STACK, width), f32),
            pltpu.VMEM((STACK, width), f32),
            pltpu.VMEM((STACK, D), f32),
        ],
        compiler_params=params(),
        cost_estimate=cost(8 * images * SEQ * D * FF, 40 << 20, 2 * images * SEQ * FF),
        name="mlp",
    )(
        who, who, h, cot, weights, weights, down1, *[array for array, _ in sides], up2,
        vectors, vectors, vectors, vectors,
    )


def qkv_grads_kernel(
    index_ref, tokens_ref, dq_ref, dk_ref, dv_ref, low_ref, up_ref, gain_ref, shift_ref,
    low_grad_ref, grad_up_ref, grad_down_ref, grad_up_s, grad_down_s,
):
    image = pl.program_id(0)
    parts = (dq_ref, dk_ref, dv_ref)

    @pl.when(image == 0)
    def _():
        grad_up_s[...] = jnp.zeros_like(grad_up_s)
        grad_down_s[...] = jnp.zeros_like(grad_down_s)

    low = low_ref[...]
    low_grad = dot(parts[0][...], up_ref[0:D, :], NN)
    for part in (1, 2):
        low_grad += dot(parts[part][...], up_ref[part * D : (part + 1) * D, :], NN)
    low_grad = keep(low_grad, index_ref[0, image])
    low_grad_ref[...] = low_grad
    for part in range(3):
        grad_up_s[part] += dot(low, parts[part][...], TN)
    normed, _ = normalize(tokens_ref[...].astype(f32))
    a = (normed * gain_ref[...] + shift_ref[...]).astype(bf16)
    grad_down_s[...] += dot(low_grad, a, TN)

    @pl.when(image == pl.num_programs(0) - 1)
    def _():
        for part in range(3):
            grad_up_ref[part * D : (part + 1) * D, :] = grad_up_s[part].T.astype(bf16)
        grad_down_ref[...] = grad_down_s[...].T.astype(bf16)


def qkv_grads(tokens, dq, dk, dv, low, up, who, vectors):
    images = tokens.shape[0]
    return pl.pallas_call(
        qkv_grads_kernel,
        grid=(images,),
        in_specs=[smem()]
        + [image_rows()] * 4
        + [image_rows(STACK), whole((3 * D, STACK)), vector(GAIN1), vector(SHIFT1)],
        out_specs=[
            image_rows(STACK),
            pl.BlockSpec((3 * D, STACK), lambda i: (0, 0)),
            pl.BlockSpec((D, STACK), lambda i: (0, 0)),
        ],
        out_shape=[
            jax.ShapeDtypeStruct((images, SEQ, STACK), bf16),
            jax.ShapeDtypeStruct((3 * D, STACK), bf16),
            jax.ShapeDtypeStruct((D, STACK), bf16),
        ],
        scratch_shapes=[pltpu.VMEM((3, STACK, D), f32), pltpu.VMEM((STACK, D), f32)],
        compiler_params=params(),
        cost_estimate=cost(2 * images * SEQ * D * D, 12 << 20),
        name="qkv_grads",
    )(who, tokens, dq, dk, dv, low, up, vectors, vectors)


def qkv_back_kernel(count, image, *refs):
    table_ref = refs[0]
    arrays = refs[1:6]
    low_grad_ref = refs[6]
    sources = refs[7 : 7 + count]
    down_ref, gain_ref = refs[7 + count : 9 + count]
    grad_ref, dq_s, dk_s, dv_s, tokens_s, dh_s, earlier_s, row_sems, weight_s, sems = refs[-10:]
    earlier_refs = refs[9 + count : -10]
    weights = list(spread_copies(sources, 0, 3, table_ref, weight_s, sems))
    held = (tokens_s, dh_s, dq_s, dk_s, dv_s)
    rows = [
        pltpu.make_async_copy(array.at[image], into_ref, row_sems.at[number])
        for number, (array, into_ref) in enumerate(zip(arrays, held))
    ]
    before = [
        pltpu.make_async_copy(ref, earlier_s.at[number], row_sems.at[len(rows) + number])
        for number, ref in enumerate(earlier_refs)
    ]
    for part in range(3):
        rows[2 + part].start()
        for copy in weights[part::3]:
            copy.start()
    for copy in (rows[0], rows[1], *before):
        copy.start()
    da = dot(low_grad_ref[...], down_ref[...], NT)
    for part, part_s in enumerate((dq_s, dk_s, dv_s)):
        rows[2 + part].wait()
        for copy in weights[part::3]:
            copy.wait()
        da += dot(part_s[...], flat(weight_s[:, :, part * D : (part + 1) * D]), NT)
    rows[0].wait()
    normed, inverse = normalize(tokens_s[...].astype(f32))
    rows[1].wait()
    grad = dh_s[...] + norm_back(da, normed, inverse, gain_ref[...])
    if len(grad_ref.shape) == 2:
        grad_ref[...] = grad
    else:
        for number, copy in enumerate(before):
            copy.wait()
            grad_ref[:, number, :] = earlier_s[number]
        grad_ref[:, len(before), :] = grad


def qkv_back(tokens, dh, dq, dk, dv, low_grad, sources, table, down, vectors, earlier):
    images = tokens.shape[0]
    image = len(earlier)
    out = (SEQ, D) if image + 1 < images else (SEQ, images, D)
    return pl.pallas_call(
        partial(qkv_back_kernel, len(sources), image),
        grid=(1,),
        in_specs=[smem()]
        + [any_space()] * 5
        + [pl.BlockSpec((pl.Squeezed(), SEQ, STACK), lambda i: (image, 0, 0))]
        + [any_space()] * len(sources)
        + [whole((D, STACK)), vector(GAIN1)]
        + [any_space()] * image,
        out_specs=whole(out),
        out_shape=jax.ShapeDtypeStruct(out, f32),
        scratch_shapes=[pltpu.VMEM((SEQ, D), bf16)] * 4
        + [
            pltpu.VMEM((SEQ, D), f32),
            pltpu.VMEM((max(image, 1), SEQ, D), f32),
            pltpu.SemaphoreType.DMA((5 + max(image, 1),)),
        ]
        + spread_scratch(sources, 3),
        compiler_params=params(),
        cost_estimate=cost(6 * SEQ * D * D, 18 << 20),
        name="qkv_back",
    )(table, tokens, dh, dq, dk, dv, low_grad, *sources, down, vectors, *earlier)


STEPS = (16, 2, 2)


def along_x(array):
    return lax.ppermute(array, "fsdp", [(f, f ^ 1) for f in range(16)])


def along_y(array):
    return lax.ppermute(array, "fsdp", [(f, f ^ 2) for f in range(16)])


def along_z(array, shift):
    pairs = [(f, (f // 4 + shift) % 4 * 4 + f % 4) for f in range(16)]
    return lax.ppermute(array, "fsdp", pairs)


def other_core(array):
    return lax.ppermute(array, "tensor", [(0, 1), (1, 0)])


def positions():
    f = lax.axis_index("fsdp")
    t = lax.axis_index("tensor")
    z, y, x = f // 4, f // 2 % 2, f % 2
    places = [z, (z + 3) % 4, (z + 2) % 4, (z + 1) % 4, y, 1 - y, x, 1 - x, t, 1 - t]
    return jnp.stack(places).astype(jnp.int32)


def move(name, places, parts, outs, moves, room=None):
    room = room or (4 << 20) + sum(2 * math.prod(shape) for shape in outs)

    def kernel(places_ref, *refs):
        sems = refs[-1]
        copies = []
        for number, (part, out, source, target) in enumerate(moves):
            copies.append(
                pltpu.make_async_copy(
                    source(refs[part], places_ref),
                    target(refs[len(parts) + out], places_ref),
                    sems.at[number],
                )
            )
            copies[-1].start()
        for copy in copies:
            copy.wait()

    return pl.pallas_call(
        kernel,
        in_specs=[smem()] + [any_space()] * len(parts),
        out_specs=[pl.BlockSpec(memory_space=pltpu.VMEM)] * len(outs),
        out_shape=[jax.ShapeDtypeStruct(shape, bf16) for shape in outs],
        scratch_shapes=[pltpu.SemaphoreType.DMA((len(moves),))],
        compiler_params=pltpu.CompilerParams(vmem_limit_bytes=room),
        name=name,
    )(places, *parts)


def everything(ref, places):
    return ref


def after(value, *others):
    return lax.optimization_barrier((value, *others))[0]


class Piece:
    def __init__(self, shard, places, tag):
        self.shard, self.places, self.tag = shard, places, tag
        self.rows, self.half = shard.shape[0], shard.shape[1] // 2

    def send_z(self):
        self.parts = [self.shard] + [along_z(self.shard, shift) for shift in (1, 2, 3)]

    def wait_for(self, other):
        self.parts[0] = after(self.parts[0], other)

    def join_z(self):
        half = self.half
        self.a, self.b = move(
            "gather_z" + self.tag, self.places, self.parts, [(4, self.rows, half)] * 2,
            [
                (
                    shift, side,
                    lambda ref, p, side=side: ref.at[:, pl.ds(side * half, half)],
                    lambda ref, p, shift=shift: ref.at[p[shift]],
                )
                for shift in range(4)
                for side in range(2)
            ],
            room=60 << 20,
        )

    def send_half(self):
        self.parts = [self.a, along_y(self.a), self.b, along_x(self.b)]

    def join_half(self):
        self.a, self.b = move(
            "gather_yx" + self.tag, self.places, self.parts, [(4, 2, self.rows, self.half)] * 2,
            [
                (0, 0, everything, lambda ref, p: ref.at[:, p[4]]),
                (1, 0, everything, lambda ref, p: ref.at[:, p[5]]),
                (2, 1, everything, lambda ref, p: ref.at[:, p[6]]),
                (3, 1, everything, lambda ref, p: ref.at[:, p[7]]),
            ],
        )

    def send_rest(self):
        self.parts = [self.a, along_x(self.a), self.b, along_y(self.b)]

    def join_rest(self):
        (joined,) = move(
            "gather_xy" + self.tag, self.places, self.parts,
            [(2, 4, 2, 2, self.rows, self.half)],
            [
                (0, 0, everything, lambda ref, p: ref.at[0, :, :, p[6]]),
                (1, 0, everything, lambda ref, p: ref.at[0, :, :, p[7]]),
                (2, 0, everything, lambda ref, p: ref.at[1, :, p[4]]),
                (3, 0, everything, lambda ref, p: ref.at[1, :, p[5]]),
            ],
        )
        self.own = joined.reshape(2, 16, self.rows, self.half)
        self.sources = (self.own, other_core(self.own))


class SmallPiece(Piece):
    def join_z(self):
        (self.a,) = move(
            "gather_z" + self.tag, self.places, self.parts, [(4, self.rows, 2 * self.half)],
            [
                (shift, 0, everything, lambda ref, p, shift=shift: ref.at[p[shift]])
                for shift in range(4)
            ],
        )

    def send_layer(self):
        diagonal = lax.ppermute(self.a, "fsdp", [(f, f ^ 3) for f in range(16)])
        self.parts = [self.a, along_x(self.a), along_y(self.a), diagonal]

    def join_layer(self):
        half = self.half
        (joined,) = move(
            "gather_layer" + self.tag, self.places, self.parts,
            [(2, 4, 2, 2, self.rows, half)],
            [
                (
                    part, 0,
                    lambda ref, p, side=side: ref.at[:, :, pl.ds(side * half, half)],
                    lambda ref, p, side=side, y=y, x=x: ref.at[side, :, p[y], p[x]],
                )
                for part, (y, x) in enumerate(((4, 6), (4, 7), (5, 6), (5, 7)))
                for side in range(2)
            ],
        )
        self.own = joined.reshape(2, 16, self.rows, half)
        self.sources = (self.own, other_core(self.own))


def transposed(stacked):
    return stacked.reshape(STACK, -1).T


def halves(rows_by_lanes, pieces):
    rows = rows_by_lanes.shape[0]
    split = rows_by_lanes.reshape(rows, pieces, 2, -1)
    return [split[:, :, side].reshape(rows, -1) for side in range(2)]


class StepGather:
    def __init__(self, qkv_weight, out_weight, fc1_weight, fc2_weight, shards):
        rows, _, column = qkv_weight.shape
        qd, qu, od, ou, f1d, f1u, f2d, f2u = shards
        places = positions()
        t = lax.axis_index("tensor")
        qkv_a, qkv_b = halves(qkv_weight.reshape(rows, 3 * column), 3)
        out_a, out_b = halves(out_weight.T, 1)
        low1 = jnp.concatenate([qd, qu], axis=0)
        low2 = jnp.concatenate([od, ou], axis=0)
        low3 = jnp.concatenate([f1d, f2u], axis=0)
        self.piece1 = Piece(
            jnp.concatenate([qkv_a, low1[:64], qkv_b, low1[64:]], axis=1), places, "1"
        )
        self.piece2 = SmallPiece(jnp.concatenate([out_a, low2, out_b, low3], axis=1), places, "2")
        hidden = jnp.concatenate(
            [fc1_weight, fc2_weight.T, f1u[:64], f1u[64:], f2d[:64], f2d[64:]], axis=1
        )
        self.hidden = hidden
        self.places, self.column = places, column
        self.width = fc1_weight.shape[1]
        self.groups = jnp.stack([2 * t, 2 * t + 1, 2 - 2 * t, 3 - 2 * t]).astype(jnp.int32)
        self.lane = 0

    def first(self, tokens, *others):
        one, two = self.piece1, self.piece2
        one.send_z()
        one.join_z()
        hidden = after(self.hidden, one.a)
        two.shard = after(two.shard, one.a)
        self.hidden = lax.all_gather(hidden, BOTH, axis=0).reshape(16, 2, *hidden.shape)
        one.send_half()
        one.wait_for(tokens)
        one.join_half()
        one.send_rest()
        one.parts[0] = after(one.parts[0], *others)
        one.join_rest()
        lanes = pl.ds(3 * self.column // 2, STACK)
        moves = [
            m
            for source, core in ((0, 8), (1, 9))
            for m in (
                (source, 0, lambda ref, p: ref.at[0, :, pl.ds(0, 32), lanes],
                 lambda ref, p, core=core: ref.at[:, p[core]]),
                (source, 1, lambda ref, p: ref.at[0, :, pl.ds(32, 32), lanes],
                 lambda ref, p, core=core: ref.at[:, p[core], pl.ds(0, 32)]),
                (source, 1, lambda ref, p: ref.at[1, :, :, lanes],
                 lambda ref, p, core=core: ref.at[:, p[core], pl.ds(32, 64)]),
            )
        ]
        return one.sources, self.places, one.sources, moves

    def after_qkv(self, q):
        two = self.piece2
        two.shard = after(two.shard, q)
        two.send_z()
        return q

    def between_images(self, o):
        two = self.piece2
        two.wait_for(o)
        two.join_z()
        two.send_layer()
        return after(o, two.a)

    def second(self, o):
        self.piece2.wait_for(o)
        self.piece2.join_layer()
        lanes = pl.ds(self.column // 2, STACK)
        stacks = move(
            "stacks2", self.places, self.piece2.sources, [(16, 2, 32, STACK)] * 4,
            [
                (source, out,
                 lambda ref, p, out=out: ref.at[out // 2, :, pl.ds(out % 2 * 32, 32), lanes],
                 lambda ref, p, core=core: ref.at[:, p[core]])
                for source, core in ((0, 8), (1, 9))
                for out in range(4)
            ],
            room=60 << 20,
        )
        od, ou, f1d, f2u = [stack.reshape(-1, STACK) for stack in stacks]
        self.stacks = (f1d, f2u)
        return self.piece2.sources, od, ou

    def third(self):
        f1d, f2u = self.stacks
        base = 2 * self.width // STACK
        sides = [[(self.hidden, base + 2 * out + side) for side in range(2)] for out in range(2)]
        return self.hidden, f1d, sides[0], sides[1], f2u


class WholeGather:
    def __init__(self, qkv_weight, out_weight, fc1_weight, fc2_weight, shards):
        rows, _, column = qkv_weight.shape
        piece = jnp.concatenate(
            [fc1_weight, fc2_weight.T, qkv_weight.reshape(rows, 3 * column), out_weight.T],
            axis=1,
        )
        groups = lax.axis_size("tensor")
        self.joined = lax.all_gather(piece, BOTH, axis=0).reshape(-1, groups, *piece.shape)
        stacked = lax.all_gather(jnp.concatenate(shards, axis=0), BOTH, axis=0)
        self.full = []
        offset = 0
        for shard in shards:
            part = stacked[:, offset : offset + shard.shape[0]]
            self.full.append(part.reshape(-1, STACK))
            offset += shard.shape[0]
        start = 2 * fc1_weight.shape[1]
        by_group = self.joined[..., start:].transpose(1, 0, 2, 3)
        self.qkv, self.out = by_group[..., : 3 * column], by_group[..., 3 * column :]
        self.groups = jnp.arange(groups, dtype=jnp.int32)
        self.lane = 0

    def first(self, tokens, *others):
        stacks = [part.reshape(shape) for part, shape in zip(self.full[:2], STACK_SHAPES)]
        moves = [(part, part, everything, everything) for part in range(2)]
        return (self.qkv,), jnp.zeros((1,), jnp.int32), stacks, moves

    def after_qkv(self, q):
        return q

    def between_images(self, o):
        return o

    def second(self, o):
        return (self.out,), self.full[2], self.full[3]

    def third(self):
        down1, up1, down2, up2 = self.full[4:]
        view = lambda stack: [(stack.reshape(16, 2, -1, STACK), 0)]
        return self.joined, down1, view(up1), view(down2), up2


def small_call(name, kernel, places, parts, outs):
    vmem = pl.BlockSpec(memory_space=pltpu.VMEM)
    return pl.pallas_call(
        kernel,
        in_specs=[smem()] + [vmem] * len(parts),
        out_specs=[vmem] * len(outs),
        out_shape=[jax.ShapeDtypeStruct(shape, dtype) for shape, dtype in outs],
        compiler_params=pltpu.CompilerParams(vmem_limit_bytes=24 << 20),
        name=name,
    )(places, *parts)


def add(*values):
    total = values[0].astype(f32)
    for value in values[1:]:
        total += value.astype(f32)
    return total


class StepScatter:
    def __init__(self, terms, tag):
        self.places, self.tag = positions(), tag
        self.widths = [term.shape[0] // 32 for term in terms]
        self.total = sum(self.widths)
        moves = []
        offset = 0
        for number, width in enumerate(self.widths):
            for out, core in enumerate((8, 9)):
                moves.append(
                    (number, out,
                     lambda ref, p, core=core: ref.at[:, :, :, p[core]],
                     lambda ref, p, offset=offset, width=width: ref.at[
                         :, :, :, pl.ds(offset, width)])
                )
            offset += width
        split = [
            term.reshape(4, 2, 2, 2, width, STACK) for term, width in zip(terms, self.widths)
        ]
        kept, sent = move(
            "scatter_core" + tag, self.places, split, [(4, 2, 2, self.total, STACK)] * 2, moves,
            room=60 << 20,
        )
        self.parts = [kept, other_core(sent)]
        self.mark = kept

    def wait_for(self, other):
        self.parts[0] = after(self.parts[0], other)

    def layer(self):
        def kernel(p, kept, came, *outs):
            for out, y, x in zip(outs, (4, 4, 5, 5), (6, 7, 6, 7)):
                out[...] = add(kept[:, p[y], p[x]], came[:, p[y], p[x]]).astype(bf16)

        shape = ((4, self.total, STACK), bf16)
        own, to_x, to_y, to_both = small_call(
            "scatter_layer" + self.tag, kernel, self.places, self.parts, [shape] * 4
        )
        diagonal = lax.ppermute(to_both, "fsdp", [(f, f ^ 3) for f in range(16)])
        self.parts = [own, along_x(to_x), along_y(to_y), diagonal]
        self.mark = own

    def layers(self):
        def kernel(p, one, two, three, four, *outs):
            for shift, out in enumerate(outs):
                z = (p[0] + shift) % 4
                out[...] = add(one[z], two[z], three[z], four[z]).astype(out.dtype)

        own, *sends = small_call(
            "scatter_layers" + self.tag, kernel, self.places, self.parts,
            [((self.total, STACK), f32)] + [((self.total, STACK), bf16)] * 3,
        )
        self.parts = [own] + [along_z(send, shift + 1) for shift, send in enumerate(sends)]
        self.mark = own

    def finish(self):
        def kernel(p, own, first, second, third, *outs):
            value = add(own[...], first[...], second[...], third[...])
            offset = 0
            for width, out in zip(self.widths, outs):
                out[...] = value[offset : offset + width].T
                offset += width

        return small_call(
            "scatter_sum" + self.tag, kernel, self.places, self.parts,
            [((STACK, width), f32) for width in self.widths],
        )


class WholeScatter:
    def __init__(self, terms, tag):
        members = lax.axis_size(BOTH)
        packed = jnp.concatenate(
            [term.reshape(members, -1, STACK).astype(f32) for term in terms], axis=1
        )
        self.widths = [term.shape[0] // members for term in terms]
        self.summed = lax.psum_scatter(packed, BOTH, scatter_dimension=0, tiled=False)
        self.mark = terms[0]

    def wait_for(self, other):
        pass

    def layer(self):
        pass

    def layers(self):
        pass

    def finish(self):
        grads = []
        offset = 0
        for width in self.widths:
            grads.append(self.summed[offset : offset + width].T)
            offset += width
        return grads


def on_device(
    tokens,
    cotangent,
    adapter_index,
    filled,
    ln1_gain,
    ln1_shift,
    qkv_weight,
    qv_bias,
    out_weight,
    out_bias,
    ln2_gain,
    ln2_shift,
    fc1_weight,
    fc1_bias,
    fc2_weight,
    fc2_bias,
    qkv_down,
    qkv_up,
    out_down,
    out_up,
    fc1_down,
    fc1_up,
    fc2_down,
    fc2_up,
):
    images = tokens.shape[0]
    own_start = lax.axis_index("tensor") * images
    who = lax.dynamic_slice_in_dim(
        jnp.stack([adapter_index, filled]), own_start, images, 1
    )
    vectors = jnp.concatenate(
        [ln1_gain, ln1_shift, out_bias, ln2_gain, ln2_shift, fc2_bias, fc1_bias]
    ).astype(f32)[None, :]
    stack_list = (qkv_down, qkv_up, out_down, out_up, fc1_down, fc1_up, fc2_down, fc2_up)
    steps = (lax.axis_size("fsdp"), lax.axis_size("tensor"), images) == STEPS
    shards = [transposed(stacked) for stacked in stack_list]
    gather = (StepGather if steps else WholeGather)(
        qkv_weight, out_weight, fc1_weight, fc2_weight, shards
    )
    scatter = StepScatter if steps else WholeScatter
    groups = gather.groups
    tokens = untangle(tokens)
    cotangent = untangle(cotangent)
    qkv_sources, places, stacks, moves = gather.first(tokens, cotangent, vectors, who)
    q, k, v, low_one, qkv_down_full, qkv_up_full = qkv_project(
        tokens, qkv_sources, groups, places, stacks, moves, who, qv_bias, vectors
    )
    qkv_down_full = qkv_down_full.reshape(D, STACK)
    qkv_up_full = qkv_up_full.reshape(3 * D, STACK)
    q = gather.after_qkv(q)
    mixed = None
    for image in range(images):
        mixed = attend(q, k, v, image, mixed)
        if image == 0 and images > 1:
            mixed = (gather.between_images(mixed[0]), *mixed[1:])
    o, *kept = mixed
    out_sources, out_down_full, out_up_full = gather.second(o)
    h, low_out = out_project(
        tokens, o, out_sources, gather.lane, groups, out_down_full, out_up_full, who, vectors
    )
    mlp_weights, *stacks = gather.third()
    outputs, dh, grad_up2, grad_down2, grad_up1, grad_down1 = mlp(
        h, cotangent, mlp_weights, *stacks, who, vectors
    )
    do, grad_out_up, grad_out_down = out_back(
        dh, o, low_out, out_sources, gather.lane, groups, out_down_full, out_up_full, who
    )
    early = scatter(
        [grad_out_down, grad_out_up, grad_down1, grad_up1, grad_down2, grad_up2], "1"
    )
    do = after(do, early.mark)
    grads = None
    for image in range(images):
        grads = attend_back(q, k, v, do, o, kept, image, grads)
        if image == 0:
            early.wait_for(grads[0])
            early.layer()
            grads = (after(grads[0], early.mark), *grads[1:])
    dq, dk, dv = grads
    early.wait_for(dq)
    early.layers()
    dq = after(dq, early.mark)
    low_grad, grad_qkv_up, grad_qkv_down = qkv_grads(
        tokens, dq, dk, dv, low_one, qkv_up_full, who, vectors
    )
    late = scatter([grad_qkv_down, grad_qkv_up], "2")
    early_grads = early.finish()
    low_grad = after(low_grad, late.mark, early_grads[0])
    rows_grads = []
    for image in range(images):
        rows_grads.append(
            qkv_back(
                tokens, dh, dq, dk, dv, low_grad, qkv_sources, groups, qkv_down_full,
                vectors, rows_grads,
            )
        )
        if image == 0:
            late.wait_for(rows_grads[0])
            late.layer()
            rows_grads[0] = after(rows_grads[0], late.mark)
    input_grad = rows_grads[-1].transpose(1, 0, 2)
    late.layers()
    grads = [grad.reshape(ADAPTERS, RANK, -1) for grad in (*late.finish(), *early_grads)]
    return (outputs.transpose(1, 0, 2), input_grad, *grads)


def solution(mesh):
    images = P(BOTH, None, None)
    stacked = P(None, None, BOTH)
    in_specs = (
        images, images, P("fsdp"), P("fsdp"), P(), P(), P("fsdp", None, "tensor"), P(),
        P("tensor", "fsdp"), P(), P(), P(), P("fsdp", "tensor"), P(), P("tensor", "fsdp"), P(),
    ) + (stacked,) * 8
    out_specs = (images, images) + (stacked,) * 8
    return jax.shard_map(
        on_device, mesh=mesh, in_specs=in_specs, out_specs=out_specs, check_vma=False
    )
```

profile of v0, /device:TPU:0, one launch (start us, length us, event | category | flops | bytes accessed | tf_op | source)
XLA Modules:
  0.0 392.7 jit_solution(1284948718206951145)
XLA Ops:
  10.1 3.1 collective-permute-start
  19.2 2.7 collective-permute-done.refs_1_
  21.9 9.0 %collective-permute-done.1.refs_2_ = bf16[64,1792]{1,0:T(8,128)(2,1)} collective-permute-done((bf16[64,1792]{1,0:T(8,128)(2,1)S(1)}, bf16[64,1792]{1,0:T(8,128)(2,1)}, u32[]{:S(2)}, u32[]{:S(2)}) %collective-permute-start.1) | collective-permute-done | bytes 229408 | tf_op jit(solution)/shard_map/ppermute | solution.py:781
  30.9 2.9 gather_z1.1
  37.0 5.2 %untangle.2.refs_3_.tokens_ref.refs_1_ = bf16[2,577,1024]{2,1,0:T(8,128)(2,1)S(1)} custom-call(bf16[577,2,1024]{2,1,0:T(2,128)(2,1)S(1)} %bitcast.82), custom_call_target="tpu_custom_call" | custom-call | tf_op jit(solution)/shard_map/untangle/pallas_call | solution.py:111
  43.6 2.9 collective-permute-done.3.refs_1_
  53.4 5.2 %untangle.3.refs_3_ = bf16[2,577,1024]{2,1,0:T(8,128)(2,1)S(1)} custom-call(bf16[577,2,1024]{2,1,0:T(2,128)(2,1)S(1)} %bitcast.83), custom_call_target="tpu_custom_call" | custom-call | tf_op jit(solution)/shard_map/untangle/pallas_call | solution.py:111
  60.6 15.1 %collective-permute-done.5.refs_1_ = bf16[4,2,64,896]{3,2,1,0:T(8,128)(2,1)S(1)} collective-permute-done((bf16[4,2,64,896]{3,2,1,0:T(8,128)(2,1)S(1)}, bf16[4,2,64,896]{3,2,1,0:T(8,128)(2,1)S(1)}, u32[]{:S(2)}, u32[]{:S(2)}) %collective-permute-start.5) | collective-permute-done | bytes 917536 | tf_op jit(solution)/shard_map/ppermute | solution.py:772
  76.3 3.8 gather_xy1.1
  81.4 5.6 %collective-permute-done.7.refs_5_.refs_7_.refs_8_ = bf16[2,16,64,896]{3,2,1,0:T(8,128)(2,1)} collective-permute-done((bf16[2,16,64,896]{3,2,1,0:T(8,128)(2,1)}, bf16[2,16,64,896]{3,2,1,0:T(8,128)(2,1)}, u32[]{:S(2)}, u32[]{:S(2)}) %collective-permute-start.7) | collective-permute-done | bytes 3670048 | tf_op jit(solution)/shard_map/ppermute | solution.py:785
  87.0 18.6 %qkv_project.1 = (bf16[2,577,1024]{2,1,0:T(8,128)(2,1)}, bf16[2,577,1024]{2,1,0:T(8,128)(2,1)}, bf16[2,577,1024]{2,1,0:T(8,128)(2,1)}, bf16[2,577,128]{2,1,0:T(8...) custom-call(s32[4]{0:T(128)} %pad_add_fusion.1.refs_0_, s32[10]{0:T(128)} %stack.97.places_ref.refs_1_.p, ...), custom_call_target="tpu_custom_call" | custom-call | flops 7260340224 | bytes 20971520 | tf_op jit(solution)/shard_map/qkv_project/pallas_call | solution.py:268
  105.6 6.3 %collective-permute-start.10 = (bf16[64,768]{1,0:T(8,128)(2,1)S(1)}, bf16[64,768]{1,0:T(8,128)(2,1)S(1)}, u32[]{:S(2)}, u32[]{:S(2)}) collective-permute-start(bf16[64,768]{1,0:T(8,128)(2,1)S(1)} %maximum_maximum_fusion.refs_0_), channel_id=1, source_target_pairs={{0,24},{2,26},{4,28},{6,30},{8,0},{10,2},{12,4},{14,6},{16,8},{18,... | collective-permute-start | bytes 294920 | tf_op jit(solution)/shard_map/ppermute | solution.py:781
  112.0 5.4 %collective-permute-start.8 = (bf16[64,768]{1,0:T(8,128)(2,1)S(1)}, bf16[64,768]{1,0:T(8,128)(2,1)S(1)}, u32[]{:S(2)}, u32[]{:S(2)}) collective-permute-start(bf16[64,768]{1,0:T(8,128)(2,1)S(1)} %maximum_maximum_fusion.refs_0_), channel_id=1, source_target_pairs={{0,8},{2,10},{4,12},{6,14},{8,16},{10,18},{12,20},{14,22},{16,24},... | collective-permute-start | bytes 294920 | tf_op jit(solution)/shard_map/ppermute | solution.py:781
  118.8 16.5 %attend.2 = (bf16[2,577,1024]{2,1,0:T(8,128)(2,1)}, bf16[32,577,577]{2,1,0:T(8,128)(2,1)}, f32[2,577,1024]{2,1,0:T(8,128)}) custom-call(bf16[2,577,1024]{2,1,0:T(8,128)(2,1)} %get-tuple-element.100.q_ref.refs_0_, bf16[2,577,1024]{2,1,0:T(8,128)(2,1)} %get-tuple-element.101.k_ref.refs_1_, bf16[2,577,1024]{2,1,0:T(8,128)(2,1)} %get-tuple-element.102.v_ref.refs_2_), custom_call_target="tpu_custom_call" | custom-call | flops 5454708736 | bytes 20971520 | tf_op jit(solution)/shard_map/attend/pallas_call | solution.py:318
  135.3 3.6 collective-permute-done.9.refs_2_
  143.6 16.2 %attend.3 = (bf16[2,577,1024]{2,1,0:T(8,128)(2,1)}, bf16[32,577,577]{2,1,0:T(8,128)(2,1)}, f32[2,577,1024]{2,1,0:T(8,128)}) custom-call(bf16[2,577,1024]{2,1,0:T(8,128)(2,1)} %get-tuple-element.100.q_ref.refs_0_, bf16[2,577,1024]{2,1,0:T(8,128)(2,1)} %get-tuple-element.101.k_ref.refs_1_, ...), custom_call_target="tpu_custom_call", output_to_operand_aliasing={{0}: (3, {}), {1}: (4, {}), {2}: (5, {})} | custom-call | flops 5454708736 | bytes 20971520 | tf_op jit(solution)/shard_map/attend/pallas_call | solution.py:322
  161.9 3.4 collective-permute-done.14.refs_1_.refs_6_.refs_7_
  166.6 3.0 stacks2.1
  169.6 10.7 %out_project.1 = (f32[2,577,1024]{2,1,0:T(8,128)}, bf16[2,577,128]{2,1,0:T(8,128)(2,1)}) custom-call(s32[4]{0:T(128)} %pad_add_fusion.1.refs_0_, s32[2,2]{1,0:T(2,128)} %constant_dynamic-slice_fusion.refs_2_.refs_1_.refs_0_.index_ref, s32[2,2]{1,0:T(2,128)} %constant_dynamic-slice_fusion.refs_2_.refs_1_.refs_0_.index_ref, bf16[2,577,1024]{2,1,0:T(8,128)(2,1)} %copy-done, ...), custom_call_target="tpu_custom_call" | custom-call | flops 2420113408 | bytes 12582912 | tf_op jit(solution)/shard_map/out_project/pallas_call | solution.py:402
  180.3 76.8 %mlp.1 = (bf16[577,2,1024]{2,1,0:T(2,128)(2,1)}, f32[2,577,1024]{2,1,0:T(8,128)}, bf16[1024,128]{1,0:T(8,128)(2,1)}, bf16[4096,128]{1,0:T(8,128)(2,1)}, bf16[409...) custom-call(s32[2,2]{1,0:T(2,128)} %constant_dynamic-slice_fusion.refs_2_.refs_1_.refs_0_.index_ref, ...), custom_call_target="tpu_custom_call" | custom-call | flops 38721814528 | bytes 41943040 | tf_op jit(solution)/shard_map/mlp/pallas_call | solution.py:589
  257.1 10.6 %out_back.1 = (bf16[2,577,1024]{2,1,0:T(8,128)(2,1)}, bf16[1024,128]{1,0:T(8,128)(2,1)}, bf16[1024,128]{1,0:T(8,128)(2,1)}) custom-call(s32[4]{0:T(128)} %pad_add_fusion.1.refs_0_, s32[2,2]{1,0:T(2,128)} %constant_dynamic-slice_fusion.refs_2_.refs_1_.refs_0_.index_ref, s32[2,2]{1,0:T(2,128)} %constant_dynamic-slice_fusion.refs_2_.refs_1_.refs_0_.index_ref, ...), custom_call_target="tpu_custom_call" | custom-call | flops 2420113408 | bytes 12582912 | tf_op jit(solution)/shard_map/out_back/pallas_call | solution.py:457
  267.7 4.4 %scatter_core1.1 = (bf16[4,2,2,384,128]{4,3,2,1,0:T(8,128)(2,1)}, bf16[4,2,2,384,128]{4,3,2,1,0:T(8,128)(2,1)}) custom-call(s32[10]{0:T(128)} %stack.97.places_ref.refs_1_.p, bf16[4,2,2,2,32,128]{5,4,3,2,1,0:T(8,128)(2,1)} %bitcast.103, bf16[4,2,2,2,32,128]{5,4,3,2,1,0:T(8,128)(2,1)} %bitcast.102, bf16[4,2,2,2,32,128]{5,4,3,2,1,0:T(8,128)(2,1)} %bitcast.101, ...), custom_call_target="tpu_custom_call" | custom-call | tf_op jit(solution)/shard_map/scatter_core1/pallas_call | solution.py:814
  272.2 20.2 %attend_back.2 = (bf16[2,577,1024]{2,1,0:T(8,128)(2,1)}, bf16[2,577,1024]{2,1,0:T(8,128)(2,1)}, bf16[2,577,1024]{2,1,0:T(8,128)(2,1)}) custom-call(bf16[2,577,1024]{2,1,0:T(8,128)(2,1)} %get-tuple-element.100.q_ref.refs_0_, bf16[2,577,1024]{2,1,0:T(8,128)(2,1)} %get-tuple-element.101.k_ref.refs_1_, bf16[2,577,1024]{2,1,0:T(8,128)(2,1)} %get-tuple-element.102.v_ref.refs_2_, ...), custom_call_target="tpu_custom_call" | custom-call | flops 10909417472 | bytes 25165824 | tf_op jit(solution)/shard_map/attend_back/pallas_call | solution.py:318
  297.7 20.1 %attend_back.3 = (bf16[2,577,1024]{2,1,0:T(8,128)(2,1)}, bf16[2,577,1024]{2,1,0:T(8,128)(2,1)}, bf16[2,577,1024]{2,1,0:T(8,128)(2,1)}) custom-call(bf16[2,577,1024]{2,1,0:T(8,128)(2,1)} %get-tuple-element.100.q_ref.refs_0_, bf16[2,577,1024]{2,1,0:T(8,128)(2,1)} %get-tuple-element.101.k_ref.refs_1_, ...), custom_call_target="tpu_custom_call", output_to_operand_aliasing={{0}: (7, {}), {1}: (8, {}), {2}: (9, {})} | custom-call | flops 10909417472 | bytes 25165824 | tf_op jit(solution)/shard_map/attend_back/pallas_call | solution.py:322
  318.6 10.4 %qkv_grads.1 = (bf16[2,577,128]{2,1,0:T(8,128)(2,1)}, bf16[3072,128]{1,0:T(8,128)(2,1)}, bf16[1024,128]{1,0:T(8,128)(2,1)}) custom-call(s32[2,2]{1,0:T(2,128)} %constant_dynamic-slice_fusion.refs_2_.refs_1_.refs_0_.index_ref, bf16[2,577,1024]{2,1,0:T(8,128)(2,1)} %copy-done, bf16[2,577,1024]{2,1,0:T(8,128)(2,1)} %get-tuple-element.145.dq_ref.refs_3_, ...), custom_call_target="tpu_custom_call" | custom-call | flops 2420113408 | bytes 12582912 | tf_op jit(solution)/shard_map/qkv_grads/pallas_call | solution.py:674
  329.1 3.0 scatter_core2.1
  334.1 2.8 collective-permute-start.20
  340.0 3.9 collective-permute-done.20.second
  345.3 11.3 %qkv_back.2.refs_11_ = f32[577,1024]{1,0:T(8,128)} custom-call(s32[4]{0:T(128)} %pad_add_fusion.1.refs_0_, bf16[2,577,1024]{2,1,0:T(8,128)(2,1)} %copy-done, f32[2,577,1024]{2,1,0:T(8,128)} %get-tuple-element.119.refs_3_.refs_2_, bf16[2,577,1024]{2,1,0:T(8,128)(2,1)} %get-tuple-element.145.dq_ref.refs_3_, ...), custom_call_target="tpu_custom_call" | custom-call | flops 3630170112 | bytes 18874368 | tf_op jit(solution)/shard_map/qkv_back/pallas_call | solution.py:744
  360.8 2.9 collective-permute-done.23.two
  366.3 2.7 collective-permute-start.26
  371.7 12.6 %qkv_back.3 = f32[577,2,1024]{2,1,0:T(2,128)} custom-call(s32[4]{0:T(128)} %pad_add_fusion.1.refs_0_, bf16[2,577,1024]{2,1,0:T(8,128)(2,1)} %copy-done, f32[2,577,1024]{2,1,0:T(8,128)} %get-tuple-element.119.refs_3_.refs_2_, bf16[2,577,1024]{2,1,0:T(8,128)(2,1)} %get-tuple-element.145.dq_ref.refs_3_, ...), custom_call_target="tpu_custom_call" | custom-call | flops 3630170112 | bytes 18874368 | tf_op jit(solution)/shard_map/qkv_back/pallas_call | solution.py:744
  (162 shorter events, 56.7 us)
Async XLA Ops:
  7.2 173.1 %all-gather.3.cloned.1.call-start = ((), (), s32[]{:S(2)}) async-start(), calls=%async_computation | async-start | bytes 19464192 | tf_op jit(solution)/shard_map/all_gather | solution.py:965
  8.6 28.4 %copy-start.3 = (bf16[2,577,1024]{2,0,1:T(2,128)(2,1)S(1)}, bf16[2,577,1024]{2,0,1:T(2,128)(2,1)}, u32[]{:S(2)}) copy-start(bf16[2,577,1024]{2,0,1:T(2,128)(2,1)} %param.24) | copy-start | bytes 7090180
  10.1 11.8 %collective-permute-start = (bf16[64,1792]{1,0:T(8,128)(2,1)S(1)}, bf16[64,1792]{1,0:T(8,128)(2,1)}, u32[]{:S(2)}, u32[]{:S(2)}) collective-permute-start(bf16[64,1792]{1,0:T(8,128)(2,1)S(1)} %fusion.2.refs_0_), channel_id=1, source_target_pairs={{0,8},{2,10},{4,12},{6,14},{8,16},{10,18},{12,20},{14,22},{16,24},... | collective-permute-start | bytes 688136 | tf_op jit(solution)/shard_map/ppermute | solution.py:781
  13.2 17.7 %collective-permute-start.1 = (bf16[64,1792]{1,0:T(8,128)(2,1)S(1)}, bf16[64,1792]{1,0:T(8,128)(2,1)}, u32[]{:S(2)}, u32[]{:S(2)}) collective-permute-start(bf16[64,1792]{1,0:T(8,128)(2,1)S(1)} %fusion.2.refs_0_), channel_id=1, source_target_pairs={{0,16},{2,18},{4,20},{6,22},{8,24},{10,26},{12,28},{14,30},{16,0},... | collective-permute-start | bytes 688136 | tf_op jit(solution)/shard_map/ppermute | solution.py:781
  15.8 15.1 %collective-permute-start.2 = (bf16[64,1792]{1,0:T(8,128)(2,1)S(1)}, bf16[64,1792]{1,0:T(8,128)(2,1)}, u32[]{:S(2)}, u32[]{:S(2)}) collective-permute-start(bf16[64,1792]{1,0:T(8,128)(2,1)S(1)} %fusion.2.refs_0_), channel_id=1, source_target_pairs={{0,24},{2,26},{4,28},{6,30},{8,0},{10,2},{12,4},{14,6},{16,8},{18,... | collective-permute-start | bytes 688136 | tf_op jit(solution)/shard_map/ppermute | solution.py:781
  33.9 12.6 %collective-permute-start.3 = (bf16[4,64,896]{2,1,0:T(8,128)(2,1)}, bf16[4,64,896]{2,1,0:T(8,128)(2,1)S(1)}, u32[]{:S(2)}, u32[]{:S(2)}) collective-permute-start(bf16[4,64,896]{2,1,0:T(8,128)(2,1)} %get-tuple-element.95.refs_0_), channel_id=1, source_target_pairs={{0,4},{2,6},{4,0},{6,2},{8,12},{10,14},{12,8},{14,10},{16,20},{18,... | collective-permute-start | bytes 1376264 | tf_op jit(solution)/shard_map/ppermute | solution.py:776
  35.5 12.3 %collective-permute-start.4 = (bf16[4,64,896]{2,1,0:T(8,128)(2,1)}, bf16[4,64,896]{2,1,0:T(8,128)(2,1)S(1)}, u32[]{:S(2)}, u32[]{:S(2)}) collective-permute-start(bf16[4,64,896]{2,1,0:T(8,128)(2,1)} %get-tuple-element.96.refs_2_), channel_id=1, source_target_pairs={{0,2},{2,0},{4,6},{6,4},{8,10},{10,8},{12,14},{14,12},{16,18},{18,... | collective-permute-start | bytes 1376264 | tf_op jit(solution)/shard_map/ppermute | solution.py:772
  48.9 26.9 %collective-permute-start.5 = (bf16[4,2,64,896]{3,2,1,0:T(8,128)(2,1)S(1)}, bf16[4,2,64,896]{3,2,1,0:T(8,128)(2,1)S(1)}, u32[]{:S(2)}, u32[]{:S(2)}) collective-permute-start(bf16[4,2,64,896]{3,2,1,0:T(8,128)(2,1)S(1)} %get-tuple-element.98.refs_0_), channel_id=1, source_target_pairs={{0,2},{2,0},{4,6},{6,4},{8,10},{10,8},{12,14},{14,12},{16,18},{18,... | collective-permute-start | bytes 2752520 | tf_op jit(solution)/shard_map/ppermute | solution.py:772
  50.4 25.9 %collective-permute-start.6 = (bf16[4,2,64,896]{3,2,1,0:T(8,128)(2,1)S(1)}, bf16[4,2,64,896]{3,2,1,0:T(8,128)(2,1)}, u32[]{:S(2)}, u32[]{:S(2)}) collective-permute-start(bf16[4,2,64,896]{3,2,1,0:T(8,128)(2,1)S(1)} %get-tuple-element.99.refs_2_), channel_id=1, source_target_pairs={{0,4},{2,6},{4,0},{6,2},{8,12},{10,14},{12,8},{14,10},{16,20},{18,... | collective-permute-start | bytes 2752520 | tf_op jit(solution)/shard_map/ppermute | solution.py:776
  80.1 6.8 %collective-permute-start.7 = (bf16[2,16,64,896]{3,2,1,0:T(8,128)(2,1)}, bf16[2,16,64,896]{3,2,1,0:T(8,128)(2,1)}, u32[]{:S(2)}, u32[]{:S(2)}) collective-permute-start(bf16[2,16,64,896]{3,2,1,0:T(8,128)(2,1)} %bitcast.22.refs_4_.refs_6_.refs_7_), channel_id=1, source_target_pairs={{0,1},{1,0},{2,3},{3,2},{4,5},{5,4},{6,7},{7,6},{8,9},{9,8},{10,11... | collective-permute-start | bytes 11010056 | tf_op jit(solution)/shard_map/ppermute | solution.py:785
  105.6 29.7 %collective-permute-start.10 = (bf16[64,768]{1,0:T(8,128)(2,1)S(1)}, bf16[64,768]{1,0:T(8,128)(2,1)S(1)}, u32[]{:S(2)}, u32[]{:S(2)}) collective-permute-start(bf16[64,768]{1,0:T(8,128)(2,1)S(1)} %maximum_maximum_fusion.refs_0_), channel_id=1, source_target_pairs={{0,24},{2,26},{4,28},{6,30},{8,0},{10,2},{12,4},{14,6},{16,8},{18,... | collective-permute-start | bytes 294920 | tf_op jit(solution)/shard_map/ppermute | solution.py:781
  112.0 23.3 %collective-permute-start.8 = (bf16[64,768]{1,0:T(8,128)(2,1)S(1)}, bf16[64,768]{1,0:T(8,128)(2,1)S(1)}, u32[]{:S(2)}, u32[]{:S(2)}) collective-permute-start(bf16[64,768]{1,0:T(8,128)(2,1)S(1)} %maximum_maximum_fusion.refs_0_), channel_id=1, source_target_pairs={{0,8},{2,10},{4,12},{6,14},{8,16},{10,18},{12,20},{14,22},{16,24},... | collective-permute-start | bytes 294920 | tf_op jit(solution)/shard_map/ppermute | solution.py:781
  117.4 21.5 %collective-permute-start.9 = (bf16[64,768]{1,0:T(8,128)(2,1)S(1)}, bf16[64,768]{1,0:T(8,128)(2,1)S(1)}, u32[]{:S(2)}, u32[]{:S(2)}) collective-permute-start(bf16[64,768]{1,0:T(8,128)(2,1)S(1)} %maximum_maximum_fusion.refs_0_), channel_id=1, source_target_pairs={{0,16},{2,18},{4,20},{6,22},{8,24},{10,26},{12,28},{14,30},{16,0},... | collective-permute-start | bytes 294920 | tf_op jit(solution)/shard_map/ppermute | solution.py:781
  140.0 19.8 %collective-permute-start.11 = (bf16[4,64,768]{2,1,0:T(8,128)(2,1)S(1)}, bf16[4,64,768]{2,1,0:T(8,128)(2,1)S(1)}, u32[]{:S(2)}, u32[]{:S(2)}) collective-permute-start(bf16[4,64,768]{2,1,0:T(8,128)(2,1)S(1)} %gather_z2.1.refs_0_), channel_id=1, source_target_pairs={{0,2},{2,0},{4,6},{6,4},{8,10},{10,8},{12,14},{14,12},{16,18},{18,... | collective-permute-start | bytes 1179656 | tf_op jit(solution)/shard_map/ppermute | solution.py:772
  141.6 18.3 %collective-permute-start.12 = (bf16[4,64,768]{2,1,0:T(8,128)(2,1)S(1)}, bf16[4,64,768]{2,1,0:T(8,128)(2,1)S(1)}, u32[]{:S(2)}, u32[]{:S(2)}) collective-permute-start(bf16[4,64,768]{2,1,0:T(8,128)(2,1)S(1)} %gather_z2.1.refs_0_), channel_id=1, source_target_pairs={{0,4},{2,6},{4,0},{6,2},{8,12},{10,14},{12,8},{14,10},{16,20},{18,... | collective-permute-start | bytes 1179656 | tf_op jit(solution)/shard_map/ppermute | solution.py:776
  141.6 19.4 %collective-permute-start.13 = (bf16[4,64,768]{2,1,0:T(8,128)(2,1)S(1)}, bf16[4,64,768]{2,1,0:T(8,128)(2,1)S(1)}, u32[]{:S(2)}, u32[]{:S(2)}) collective-permute-start(bf16[4,64,768]{2,1,0:T(8,128)(2,1)S(1)} %gather_z2.1.refs_0_), channel_id=1, source_target_pairs={{0,6},{2,4},{4,2},{6,0},{8,14},{10,12},{12,10},{14,8},{16,22},{18,... | collective-permute-start | bytes 1179656 | tf_op jit(solution)/shard_map/ppermute | solution.py:903
  161.8 3.5 collective-permute-start.14
  272.0 20.4 %collective-permute-start.15 = (bf16[4,2,2,384,128]{4,3,2,1,0:T(8,128)(2,1)}, bf16[4,2,2,384,128]{4,3,2,1,0:T(8,128)(2,1)S(1)}, u32[]{:S(2)}, u32[]{:S(2)}) collective-permute-start(bf16[4,2,2,384,128]{4,3,2,1,0:T(8,128)(2,1)} %get-tuple-element.134), channel_id=1, source_target_pairs={{0,1},{1,0},{2,3},{3,2},{4,5},{5,4},{6,7},{7,6},{8,9},{9,8},{10,11... | collective-permute-start | bytes 4718600 | tf_op jit(solution)/shard_map/ppermute | solution.py:785
  294.2 23.6 %collective-permute-start.16 = (bf16[4,384,128]{2,1,0:T(8,128)(2,1)}, bf16[4,384,128]{2,1,0:T(8,128)(2,1)S(1)}, u32[]{:S(2)}, u32[]{:S(2)}) collective-permute-start(bf16[4,384,128]{2,1,0:T(8,128)(2,1)} %get-tuple-element.141), channel_id=1, source_target_pairs={{0,2},{2,0},{4,6},{6,4},{8,10},{10,8},{12,14},{14,12},{16,18},{18,... | collective-permute-start | bytes 1179656 | tf_op jit(solution)/shard_map/ppermute | solution.py:772
  294.6 23.2 %collective-permute-start.17 = (bf16[4,384,128]{2,1,0:T(8,128)(2,1)}, bf16[4,384,128]{2,1,0:T(8,128)(2,1)S(1)}, u32[]{:S(2)}, u32[]{:S(2)}) collective-permute-start(bf16[4,384,128]{2,1,0:T(8,128)(2,1)} %get-tuple-element.142), channel_id=1, source_target_pairs={{0,4},{2,6},{4,0},{6,2},{8,12},{10,14},{12,8},{14,10},{16,20},{18,... | collective-permute-start | bytes 1179656 | tf_op jit(solution)/shard_map/ppermute | solution.py:776
  296.3 21.5 %collective-permute-start.18 = (bf16[4,384,128]{2,1,0:T(8,128)(2,1)S(1)}, bf16[4,384,128]{2,1,0:T(8,128)(2,1)S(1)}, u32[]{:S(2)}, u32[]{:S(2)}) collective-permute-start(bf16[4,384,128]{2,1,0:T(8,128)(2,1)S(1)} %get-tuple-element.143), channel_id=1, source_target_pairs={{0,6},{2,4},{4,2},{6,0},{8,14},{10,12},{12,10},{14,8},{16,22},{18,... | collective-permute-start | bytes 1179656 | tf_op jit(solution)/shard_map/ppermute | solution.py:1125
  318.6 25.3 %copy-start.12 = (s32[10]{0:T(128)S(1)}, s32[10]{0:T(128)}, u32[]{:S(2)}) copy-start(s32[10]{0:T(128)} %stack.97.places_ref.refs_1_.p) | copy-start | bytes 124
  332.1 24.5 %collective-permute-start.22 = (bf16[4,2,2,128,128]{4,3,2,1,0:T(8,128)(2,1)}, bf16[4,2,2,128,128]{4,3,2,1,0:T(8,128)(2,1)S(1)}, u32[]{:S(2)}, u32[]{:S(2)}) collective-permute-start(bf16[4,2,2,128,128]{4,3,2,1,0:T(8,128)(2,1)} %get-tuple-element.161), channel_id=1, source_target_pairs={{0,1},{1,0},{2,3},{3,2},{4,5},{5,4},{6,7},{7,6},{8,9},{9,8},{10,11... | collective-permute-start | bytes 1572872 | tf_op jit(solution)/shard_map/ppermute | solution.py:785
  332.1 7.9 %collective-permute-start.19 = (bf16[384,128]{1,0:T(8,128)(2,1)S(1)}, bf16[384,128]{1,0:T(8,128)(2,1)S(1)}, u32[]{:S(2)}, u32[]{:S(2)}) collective-permute-start(bf16[384,128]{1,0:T(8,128)(2,1)S(1)} %get-tuple-element.154), channel_id=1, source_target_pairs={{0,8},{2,10},{4,12},{6,14},{8,16},{10,18},{12,20},{14,22},{16,24},... | collective-permute-start | bytes 294920 | tf_op jit(solution)/shard_map/ppermute | solution.py:781
  334.1 9.9 %collective-permute-start.20 = (bf16[384,128]{1,0:T(8,128)(2,1)S(1)}, bf16[384,128]{1,0:T(8,128)(2,1)S(1)}, u32[]{:S(2)}, u32[]{:S(2)}) collective-permute-start(bf16[384,128]{1,0:T(8,128)(2,1)S(1)} %get-tuple-element.155), channel_id=1, source_target_pairs={{0,16},{2,18},{4,20},{6,22},{8,24},{10,26},{12,28},{14,30},{16,0},... | collective-permute-start | bytes 294920 | tf_op jit(solution)/shard_map/ppermute | solution.py:781
  336.8 7.1 %collective-permute-start.21 = (bf16[384,128]{1,0:T(8,128)(2,1)S(1)}, bf16[384,128]{1,0:T(8,128)(2,1)S(1)}, u32[]{:S(2)}, u32[]{:S(2)}) collective-permute-start(bf16[384,128]{1,0:T(8,128)(2,1)S(1)} %get-tuple-element.156), channel_id=1, source_target_pairs={{0,24},{2,26},{4,28},{6,30},{8,0},{10,2},{12,4},{14,6},{16,8},{18,... | collective-permute-start | bytes 294920 | tf_op jit(solution)/shard_map/ppermute | solution.py:781
  357.3 6.4 %collective-permute-start.23 = (bf16[4,128,128]{2,1,0:T(8,128)(2,1)S(1)}, bf16[4,128,128]{2,1,0:T(8,128)(2,1)S(1)}, u32[]{:S(2)}, u32[]{:S(2)}) collective-permute-start(bf16[4,128,128]{2,1,0:T(8,128)(2,1)S(1)} %get-tuple-element.164), channel_id=1, source_target_pairs={{0,2},{2,0},{4,6},{6,4},{8,10},{10,8},{12,14},{14,12},{16,18},{18,... | collective-permute-start | bytes 393224 | tf_op jit(solution)/shard_map/ppermute | solution.py:772
  357.4 8.3 %collective-permute-start.24 = (bf16[4,128,128]{2,1,0:T(8,128)(2,1)S(1)}, bf16[4,128,128]{2,1,0:T(8,128)(2,1)S(1)}, u32[]{:S(2)}, u32[]{:S(2)}) collective-permute-start(bf16[4,128,128]{2,1,0:T(8,128)(2,1)S(1)} %get-tuple-element.165), channel_id=1, source_target_pairs={{0,4},{2,6},{4,0},{6,2},{8,12},{10,14},{12,8},{14,10},{16,20},{18,... | collective-permute-start | bytes 393224 | tf_op jit(solution)/shard_map/ppermute | solution.py:776
  359.0 6.7 %collective-permute-start.25 = (bf16[4,128,128]{2,1,0:T(8,128)(2,1)S(1)}, bf16[4,128,128]{2,1,0:T(8,128)(2,1)S(1)}, u32[]{:S(2)}, u32[]{:S(2)}) collective-permute-start(bf16[4,128,128]{2,1,0:T(8,128)(2,1)S(1)} %get-tuple-element.166), channel_id=1, source_target_pairs={{0,6},{2,4},{4,2},{6,0},{8,14},{10,12},{12,10},{14,8},{16,22},{18,... | collective-permute-start | bytes 393224 | tf_op jit(solution)/shard_map/ppermute | solution.py:1125
  366.3 18.0 %collective-permute-start.26 = (bf16[128,128]{1,0:T(8,128)(2,1)S(1)}, bf16[128,128]{1,0:T(8,128)(2,1)S(1)}, u32[]{:S(2)}, u32[]{:S(2)}) collective-permute-start(bf16[128,128]{1,0:T(8,128)(2,1)S(1)} %get-tuple-element.168), channel_id=1, source_target_pairs={{0,8},{2,10},{4,12},{6,14},{8,16},{10,18},{12,20},{14,22},{16,24},... | collective-permute-start | bytes 98312 | tf_op jit(solution)/shard_map/ppermute | solution.py:781
  369.0 15.3 %collective-permute-start.27 = (bf16[128,128]{1,0:T(8,128)(2,1)S(1)}, bf16[128,128]{1,0:T(8,128)(2,1)S(1)}, u32[]{:S(2)}, u32[]{:S(2)}) collective-permute-start(bf16[128,128]{1,0:T(8,128)(2,1)S(1)} %get-tuple-element.169), channel_id=1, source_target_pairs={{0,16},{2,18},{4,20},{6,22},{8,24},{10,26},{12,28},{14,30},{16,0},... | collective-permute-start | bytes 98312 | tf_op jit(solution)/shard_map/ppermute | solution.py:781
  369.8 14.5 %collective-permute-start.28 = (bf16[128,128]{1,0:T(8,128)(2,1)S(1)}, bf16[128,128]{1,0:T(8,128)(2,1)S(1)}, u32[]{:S(2)}, u32[]{:S(2)}) collective-permute-start(bf16[128,128]{1,0:T(8,128)(2,1)S(1)} %get-tuple-element.170), channel_id=1, source_target_pairs={{0,24},{2,26},{4,28},{6,30},{8,0},{10,2},{12,4},{14,6},{16,8},{18,... | collective-permute-start | bytes 98312 | tf_op jit(solution)/shard_map/ppermute | solution.py:781
  (32 other events, 392.4 us)
Sparse Core Ops, SparseCore 0:
  34.0 138.3 all-gather.2
where the time goes:
time: 399 us; the launch traced here: 393 us
  Pallas kernels  261 us (65%)
  waiting for transfers between devices  56.5 us (14%)
  starting transfers between devices  47.1 us (12%)
  between operations  15.1 us (4%)
  local copies, waits for them, and re-layouts  11.7 us (3%)
    pallas_call x1, Pallas kernels, mlp(): pl.pallas_call(partial(mlp_kernel, len(up1)), grid=(tiles, images), in_sp...  76.8 us
    pallas_call x2, Pallas kernels, per_image(): pl.pallas_call(kernel, grid=(HEADS // 2,), in_specs=in_specs, out_specs=o...  36.7 us
    pallas_call x2, Pallas kernels, per_image(): pl.pallas_call(into(kernel, count), grid=(HEADS // 2,), in_specs=in_specs...  36.4 us
    ppermute x12, starting transfers between devices, along_z(): return lax.ppermute(array, 'fsdp', pairs)  30.9 us
    pallas_call x2, Pallas kernels, qkv_back(): pl.pallas_call(partial(qkv_back_kernel, len(sources), image), grid=(1,),...  23.9 us
    ppermute x12, waiting for transfers between devices, along_z(): return lax.ppermute(array, 'fsdp', pairs)  21.8 us
    pallas_call x8, Pallas kernels, move(): pl.pallas_call(kernel, in_specs=[smem()] + [any_space()] * len(parts), ou...  20.1 us
    ppermute x5, waiting for transfers between devices, along_x(): return lax.ppermute(array, 'fsdp', [(f, f ^ 1) for f in range(16)])  19.2 us
  transfers between devices with their start and end apart: 30, of which 14 were waited for; matrix products, arithmetic and copies ran while one was open for 1% of the time, Pallas kernels for 38%

commit v1 on v0

--- a/solution.py
+++ b/solution.py
@@ -967,7 +967,9 @@
         one.wait_for(tokens)
         one.join_half()
         one.send_rest()
-        one.parts[0] = after(one.parts[0], *others)
+        two.send_z()
+        two.join_z()
+        one.parts[0] = after(one.parts[0], two.a, *others)
         one.join_rest()
         lanes = pl.ds(3 * self.column // 2, STACK)
         moves = [
@@ -986,16 +988,12 @@
 
     def after_qkv(self, q):
         two = self.piece2
-        two.shard = after(two.shard, q)
-        two.send_z()
+        two.a = after(two.a, q)
+        two.send_layer()
         return q
 
     def between_images(self, o):
-        two = self.piece2
-        two.wait_for(o)
-        two.join_z()
-        two.send_layer()
-        return after(o, two.a)
+        return o
 
     def second(self, o):
         self.piece2.wait_for(o)

time: 399 us -> 401 us (level)
    ppermute x5, waiting for transfers between devices: 19.2 us -> 3.91 us  [along_x(): return lax.ppermute(array, 'fsdp', [(f, f ^ 1) for f in range(16)])]
    all_gather x1, waiting for transfers between devices: 0.02 us -> 13.4 us  [first(): lax.all_gather(hidden, BOTH, axis=0).reshape(16, 2, *hidden.shape)]
    ppermute x12, waiting for transfers between devices: 21.8 us -> 26.5 us  [along_z(): return lax.ppermute(array, 'fsdp', pairs)]
where the time goes in v1:
time: 401 us; the launch traced here: 395 us
  Pallas kernels  261 us (65%)
  waiting for transfers between devices  60.5 us (15%)
  starting transfers between devices  45 us (11%)
  between operations  15.2 us (4%)
  local copies, waits for them, and re-layouts  11.7 us (3%)
    pallas_call x1, Pallas kernels, mlp(): pl.pallas_call(partial(mlp_kernel, len(up1)), grid=(tiles, images), in_sp...  76.7 us
    pallas_call x2, Pallas kernels, per_image(): pl.pallas_call(kernel, grid=(HEADS // 2,), in_specs=in_specs, out_specs=o...  36.5 us
    pallas_call x2, Pallas kernels, per_image(): pl.pallas_call(into(kernel, count), grid=(HEADS // 2,), in_specs=in_specs...  36.4 us
    ppermute x12, starting transfers between devices, along_z(): return lax.ppermute(array, 'fsdp', pairs)  28.7 us
    ppermute x12, waiting for transfers between devices, along_z(): return lax.ppermute(array, 'fsdp', pairs)  26.5 us
    pallas_call x2, Pallas kernels, qkv_back(): pl.pallas_call(partial(qkv_back_kernel, len(sources), image), grid=(1,),...  23.9 us
    pallas_call x8, Pallas kernels, move(): pl.pallas_call(kernel, in_specs=[smem()] + [any_space()] * len(parts), ou...  20.5 us
    pallas_call x1, Pallas kernels, qkv_project(): pl.pallas_call(partial(qkv_kernel, len(sources), moves), grid_spec=grid_s...  19 us
  transfers between devices with their start and end apart: 30, of which 14 were waited for; matrix products, arithmetic and copies ran while one was open for 1% of the time, Pallas kernels for 38%

profile of v1, /device:TPU:0, one launch (start us, length us, event | category | flops | bytes accessed | tf_op | source)
XLA Modules:
  0.0 395.0 jit_solution(14322385224485134945)
XLA Ops:
  10.1 3.1 collective-permute-start
  19.2 2.7 collective-permute-done.refs_1_
  21.9 9.0 %collective-permute-done.1.refs_2_ = bf16[64,1792]{1,0:T(8,128)(2,1)} collective-permute-done((bf16[64,1792]{1,0:T(8,128)(2,1)S(1)}, bf16[64,1792]{1,0:T(8,128)(2,1)}, u32[]{:S(2)}, u32[]{:S(2)}) %collective-permute-start.1) | collective-permute-done | bytes 229408 | tf_op jit(solution)/shard_map/ppermute | solution.py:781
  30.9 2.9 gather_z1.1
  37.1 5.2 %untangle.2.refs_3_.tokens_ref.refs_1_ = bf16[2,577,1024]{2,1,0:T(8,128)(2,1)S(1)} custom-call(bf16[577,2,1024]{2,1,0:T(2,128)(2,1)S(1)} %bitcast.82), custom_call_target="tpu_custom_call" | custom-call | tf_op jit(solution)/shard_map/untangle/pallas_call | solution.py:111
  43.8 2.8 collective-permute-done.3.refs_1_
  53.8 5.2 %untangle.3.refs_3_ = bf16[2,577,1024]{2,1,0:T(8,128)(2,1)S(1)} custom-call(bf16[577,2,1024]{2,1,0:T(2,128)(2,1)S(1)} %bitcast.83), custom_call_target="tpu_custom_call" | custom-call | tf_op jit(solution)/shard_map/untangle/pallas_call | solution.py:111
  60.5 9.2 %collective-permute-start.5 = (bf16[64,768]{1,0:T(8,128)(2,1)S(1)}, bf16[64,768]{1,0:T(8,128)(2,1)S(1)}, u32[]{:S(2)}, u32[]{:S(2)}) collective-permute-start(bf16[64,768]{1,0:T(8,128)(2,1)S(1)} %maximum_maximum_fusion.refs_0_), channel_id=1, source_target_pairs={{0,8},{2,10},{4,12},{6,14},{8,16},{10,18},{12,20},{14,22},{16,24},... | collective-permute-start | bytes 294920 | tf_op jit(solution)/shard_map/ppermute | solution.py:781
  73.8 7.6 %collective-permute-done.6.refs_2_ = bf16[64,768]{1,0:T(8,128)(2,1)S(1)} collective-permute-done((bf16[64,768]{1,0:T(8,128)(2,1)S(1)}, bf16[64,768]{1,0:T(8,128)(2,1)S(1)}, u32[]{:S(2)}, u32[]{:S(2)}) %collective-permute-start.6) | collective-permute-done | bytes 98336 | tf_op jit(solution)/shard_map/ppermute | solution.py:781
  82.7 4.0 %gather_xy1.1 = bf16[2,4,2,2,64,896]{5,4,3,2,1,0:T(8,128)(2,1)} custom-call(s32[10]{0:T(128)S(1)} %copy-done.9, bf16[4,2,64,896]{3,2,1,0:T(8,128)(2,1)S(1)} %get-tuple-element.97.refs_0_, bf16[4,2,64,896]{3,2,1,0:T(8,128)(2,1)} %collective-permute-done.8.refs_1_, bf16[4,2,64,896]{3,2,1,0:T(8,128)(2,1)S(1)} %get-tuple-element.98.refs_2_, ...), custom_call_target="tpu_custom_call" | custom-call | tf_op jit(solution)/shard_map/gather_xy1/pallas_call | solution.py:814
  87.4 6.1 %collective-permute-done.10.refs_5_.refs_7_.refs_8_ = bf16[2,16,64,896]{3,2,1,0:T(8,128)(2,1)} collective-permute-done((bf16[2,16,64,896]{3,2,1,0:T(8,128)(2,1)}, bf16[2,16,64,896]{3,2,1,0:T(8,128)(2,1)}, u32[]{:S(2)}, u32[]{:S(2)}) %collective-permute-start.10) | collective-permute-done | bytes 3670048 | tf_op jit(solution)/shard_map/ppermute | solution.py:785
  93.5 19.0 %qkv_project.1 = (bf16[2,577,1024]{2,1,0:T(8,128)(2,1)}, bf16[2,577,1024]{2,1,0:T(8,128)(2,1)}, bf16[2,577,1024]{2,1,0:T(8,128)(2,1)}, bf16[2,577,128]{2,1,0:T(8...) custom-call(s32[4]{0:T(128)} %pad_add_fusion.1.refs_0_, s32[10]{0:T(128)} %stack.97.places_ref.refs_1_.p, ...), custom_call_target="tpu_custom_call" | custom-call | flops 7260340224 | bytes 20971520 | tf_op jit(solution)/shard_map/qkv_project/pallas_call | solution.py:268
  116.1 16.3 %attend.2 = (bf16[2,577,1024]{2,1,0:T(8,128)(2,1)}, bf16[32,577,577]{2,1,0:T(8,128)(2,1)}, f32[2,577,1024]{2,1,0:T(8,128)}) custom-call(bf16[2,577,1024]{2,1,0:T(8,128)(2,1)} %get-tuple-element.99.q_ref.refs_0_, bf16[2,577,1024]{2,1,0:T(8,128)(2,1)} %get-tuple-element.100.k_ref.refs_1_, bf16[2,577,1024]{2,1,0:T(8,128)(2,1)} %get-tuple-element.101.v_ref.refs_2_), custom_call_target="tpu_custom_call" | custom-call | flops 5454708736 | bytes 20971520 | tf_op jit(solution)/shard_map/attend/pallas_call | solution.py:318
  132.4 16.2 %attend.3 = (bf16[2,577,1024]{2,1,0:T(8,128)(2,1)}, bf16[32,577,577]{2,1,0:T(8,128)(2,1)}, f32[2,577,1024]{2,1,0:T(8,128)}) custom-call(bf16[2,577,1024]{2,1,0:T(8,128)(2,1)} %get-tuple-element.99.q_ref.refs_0_, bf16[2,577,1024]{2,1,0:T(8,128)(2,1)} %get-tuple-element.100.k_ref.refs_1_, ...), custom_call_target="tpu_custom_call", output_to_operand_aliasing={{0}: (3, {}), {1}: (4, {}), {2}: (5, {})} | custom-call | flops 5454708736 | bytes 20971520 | tf_op jit(solution)/shard_map/attend/pallas_call | solution.py:322
  151.5 3.6 collective-permute-done.14.refs_1_.refs_6_.refs_7_
  156.4 3.0 stacks2.1
  159.4 10.5 %out_project.1 = (f32[2,577,1024]{2,1,0:T(8,128)}, bf16[2,577,128]{2,1,0:T(8,128)(2,1)}) custom-call(s32[4]{0:T(128)} %pad_add_fusion.1.refs_0_, s32[2,2]{1,0:T(2,128)} %constant_dynamic-slice_fusion.refs_2_.refs_1_.refs_0_.index_ref, s32[2,2]{1,0:T(2,128)} %constant_dynamic-slice_fusion.refs_2_.refs_1_.refs_0_.index_ref, bf16[2,577,1024]{2,1,0:T(8,128)(2,1)} %copy-done, ...), custom_call_target="tpu_custom_call" | custom-call | flops 2420113408 | bytes 12582912 | tf_op jit(solution)/shard_map/out_project/pallas_call | solution.py:402
  169.9 13.4 %all-gather.3.cloned.1.call-done = bf16[2048,4608]{1,0:T(8,128)(2,1)} async-done(((bf16[64,4608]{1,0:T(8,128)(2,1)}), bf16[2048,4608]{1,0:T(8,128)(2,1)}) %all-gather.3.cloned.1.call-update) | async-done | bytes 18874384 | tf_op jit(solution)/shard_map/all_gather | solution.py:965
  183.3 76.7 %mlp.1 = (bf16[577,2,1024]{2,1,0:T(2,128)(2,1)}, f32[2,577,1024]{2,1,0:T(8,128)}, bf16[1024,128]{1,0:T(8,128)(2,1)}, bf16[4096,128]{1,0:T(8,128)(2,1)}, bf16[409...) custom-call(s32[2,2]{1,0:T(2,128)} %constant_dynamic-slice_fusion.refs_2_.refs_1_.refs_0_.index_ref, ...), custom_call_target="tpu_custom_call" | custom-call | flops 38721814528 | bytes 41943040 | tf_op jit(solution)/shard_map/mlp/pallas_call | solution.py:589
  260.1 10.6 %out_back.1 = (bf16[2,577,1024]{2,1,0:T(8,128)(2,1)}, bf16[1024,128]{1,0:T(8,128)(2,1)}, bf16[1024,128]{1,0:T(8,128)(2,1)}) custom-call(s32[4]{0:T(128)} %pad_add_fusion.1.refs_0_, s32[2,2]{1,0:T(2,128)} %constant_dynamic-slice_fusion.refs_2_.refs_1_.refs_0_.index_ref, s32[2,2]{1,0:T(2,128)} %constant_dynamic-slice_fusion.refs_2_.refs_1_.refs_0_.index_ref, ...), custom_call_target="tpu_custom_call" | custom-call | flops 2420113408 | bytes 12582912 | tf_op jit(solution)/shard_map/out_back/pallas_call | solution.py:457
  270.7 4.4 %scatter_core1.1 = (bf16[4,2,2,384,128]{4,3,2,1,0:T(8,128)(2,1)}, bf16[4,2,2,384,128]{4,3,2,1,0:T(8,128)(2,1)}) custom-call(s32[10]{0:T(128)} %stack.97.places_ref.refs_1_.p, bf16[4,2,2,2,32,128]{5,4,3,2,1,0:T(8,128)(2,1)} %bitcast.103, bf16[4,2,2,2,32,128]{5,4,3,2,1,0:T(8,128)(2,1)} %bitcast.102, bf16[4,2,2,2,32,128]{5,4,3,2,1,0:T(8,128)(2,1)} %bitcast.101, ...), custom_call_target="tpu_custom_call" | custom-call | tf_op jit(solution)/shard_map/scatter_core1/pallas_call | solution.py:814
  275.4 20.2 %attend_back.2 = (bf16[2,577,1024]{2,1,0:T(8,128)(2,1)}, bf16[2,577,1024]{2,1,0:T(8,128)(2,1)}, bf16[2,577,1024]{2,1,0:T(8,128)(2,1)}) custom-call(bf16[2,577,1024]{2,1,0:T(8,128)(2,1)} %get-tuple-element.99.q_ref.refs_0_, bf16[2,577,1024]{2,1,0:T(8,128)(2,1)} %get-tuple-element.100.k_ref.refs_1_, bf16[2,577,1024]{2,1,0:T(8,128)(2,1)} %get-tuple-element.101.v_ref.refs_2_, ...), custom_call_target="tpu_custom_call" | custom-call | flops 10909417472 | bytes 25165824 | tf_op jit(solution)/shard_map/attend_back/pallas_call | solution.py:318
  300.8 20.1 %attend_back.3 = (bf16[2,577,1024]{2,1,0:T(8,128)(2,1)}, bf16[2,577,1024]{2,1,0:T(8,128)(2,1)}, bf16[2,577,1024]{2,1,0:T(8,128)(2,1)}) custom-call(bf16[2,577,1024]{2,1,0:T(8,128)(2,1)} %get-tuple-element.99.q_ref.refs_0_, bf16[2,577,1024]{2,1,0:T(8,128)(2,1)} %get-tuple-element.100.k_ref.refs_1_, ...), custom_call_target="tpu_custom_call", output_to_operand_aliasing={{0}: (7, {}), {1}: (8, {}), {2}: (9, {})} | custom-call | flops 10909417472 | bytes 25165824 | tf_op jit(solution)/shard_map/attend_back/pallas_call | solution.py:322
  321.8 10.4 %qkv_grads.1 = (bf16[2,577,128]{2,1,0:T(8,128)(2,1)}, bf16[3072,128]{1,0:T(8,128)(2,1)}, bf16[1024,128]{1,0:T(8,128)(2,1)}) custom-call(s32[2,2]{1,0:T(2,128)} %constant_dynamic-slice_fusion.refs_2_.refs_1_.refs_0_.index_ref, bf16[2,577,1024]{2,1,0:T(8,128)(2,1)} %copy-done, bf16[2,577,1024]{2,1,0:T(8,128)(2,1)} %get-tuple-element.141.dq_ref.refs_3_, ...), custom_call_target="tpu_custom_call" | custom-call | flops 2420113408 | bytes 12582912 | tf_op jit(solution)/shard_map/qkv_grads/pallas_call | solution.py:674
  332.2 3.0 scatter_core2.1
  337.3 2.6 collective-permute-start.21
  339.9 2.9 collective-permute-done.19.first
  342.8 3.4 collective-permute-done.20.second
  347.6 11.3 %qkv_back.2.refs_11_ = f32[577,1024]{1,0:T(8,128)} custom-call(s32[4]{0:T(128)} %pad_add_fusion.1.refs_0_, bf16[2,577,1024]{2,1,0:T(8,128)(2,1)} %copy-done, f32[2,577,1024]{2,1,0:T(8,128)} %get-tuple-element.115.refs_3_.refs_2_, bf16[2,577,1024]{2,1,0:T(8,128)(2,1)} %get-tuple-element.141.dq_ref.refs_3_, ...), custom_call_target="tpu_custom_call" | custom-call | flops 3630170112 | bytes 18874368 | tf_op jit(solution)/shard_map/qkv_back/pallas_call | solution.py:744
  363.1 2.7 collective-permute-done.23.two
  368.6 2.7 collective-permute-start.26
  373.9 12.6 %qkv_back.3 = f32[577,2,1024]{2,1,0:T(2,128)} custom-call(s32[4]{0:T(128)} %pad_add_fusion.1.refs_0_, bf16[2,577,1024]{2,1,0:T(8,128)(2,1)} %copy-done, f32[2,577,1024]{2,1,0:T(8,128)} %get-tuple-element.115.refs_3_.refs_2_, bf16[2,577,1024]{2,1,0:T(8,128)(2,1)} %get-tuple-element.141.dq_ref.refs_3_, ...), custom_call_target="tpu_custom_call" | custom-call | flops 3630170112 | bytes 18874368 | tf_op jit(solution)/shard_map/qkv_back/pallas_call | solution.py:744
  (162 shorter events, 56.5 us)
Async XLA Ops:
  7.2 176.1 %all-gather.3.cloned.1.call-start = ((), (), s32[]{:S(2)}) async-start(), calls=%async_computation | async-start | bytes 19464192 | tf_op jit(solution)/shard_map/all_gather | solution.py:965
  8.6 28.4 %copy-start.27 = (bf16[1024]{0:T(1024)(128)(2,1)S(1)}, bf16[1024]{0:T(1024)(128)(2,1)}, u32[]{:S(2)}) copy-start(bf16[1024]{0:T(1024)(128)(2,1)} %param.29) | copy-start | bytes 6148
  8.6 28.5 %copy-start.3 = (bf16[2,577,1024]{2,0,1:T(2,128)(2,1)S(1)}, bf16[2,577,1024]{2,0,1:T(2,128)(2,1)}, u32[]{:S(2)}) copy-start(bf16[2,577,1024]{2,0,1:T(2,128)(2,1)} %param.24) | copy-start | bytes 7090180
  10.1 11.8 %collective-permute-start = (bf16[64,1792]{1,0:T(8,128)(2,1)S(1)}, bf16[64,1792]{1,0:T(8,128)(2,1)}, u32[]{:S(2)}, u32[]{:S(2)}) collective-permute-start(bf16[64,1792]{1,0:T(8,128)(2,1)S(1)} %fusion.2.refs_0_), channel_id=1, source_target_pairs={{0,8},{2,10},{4,12},{6,14},{8,16},{10,18},{12,20},{14,22},{16,24},... | collective-permute-start | bytes 688136 | tf_op jit(solution)/shard_map/ppermute | solution.py:781
  13.2 17.7 %collective-permute-start.1 = (bf16[64,1792]{1,0:T(8,128)(2,1)S(1)}, bf16[64,1792]{1,0:T(8,128)(2,1)}, u32[]{:S(2)}, u32[]{:S(2)}) collective-permute-start(bf16[64,1792]{1,0:T(8,128)(2,1)S(1)} %fusion.2.refs_0_), channel_id=1, source_target_pairs={{0,16},{2,18},{4,20},{6,22},{8,24},{10,26},{12,28},{14,30},{16,0},... | collective-permute-start | bytes 688136 | tf_op jit(solution)/shard_map/ppermute | solution.py:781
  15.8 15.1 %collective-permute-start.2 = (bf16[64,1792]{1,0:T(8,128)(2,1)S(1)}, bf16[64,1792]{1,0:T(8,128)(2,1)}, u32[]{:S(2)}, u32[]{:S(2)}) collective-permute-start(bf16[64,1792]{1,0:T(8,128)(2,1)S(1)} %fusion.2.refs_0_), channel_id=1, source_target_pairs={{0,24},{2,26},{4,28},{6,30},{8,0},{10,2},{12,4},{14,6},{16,8},{18,... | collective-permute-start | bytes 688136 | tf_op jit(solution)/shard_map/ppermute | solution.py:781
  33.9 12.6 %collective-permute-start.3 = (bf16[4,64,896]{2,1,0:T(8,128)(2,1)}, bf16[4,64,896]{2,1,0:T(8,128)(2,1)S(1)}, u32[]{:S(2)}, u32[]{:S(2)}) collective-permute-start(bf16[4,64,896]{2,1,0:T(8,128)(2,1)} %get-tuple-element.93.refs_0_), channel_id=1, source_target_pairs={{0,4},{2,6},{4,0},{6,2},{8,12},{10,14},{12,8},{14,10},{16,20},{18,... | collective-permute-start | bytes 1376264 | tf_op jit(solution)/shard_map/ppermute | solution.py:776
  35.5 12.3 %collective-permute-start.4 = (bf16[4,64,896]{2,1,0:T(8,128)(2,1)}, bf16[4,64,896]{2,1,0:T(8,128)(2,1)S(1)}, u32[]{:S(2)}, u32[]{:S(2)}) collective-permute-start(bf16[4,64,896]{2,1,0:T(8,128)(2,1)} %get-tuple-element.94.refs_2_), channel_id=1, source_target_pairs={{0,2},{2,0},{4,6},{6,4},{8,10},{10,8},{12,14},{14,12},{16,18},{18,... | collective-permute-start | bytes 1376264 | tf_op jit(solution)/shard_map/ppermute | solution.py:772
  48.9 33.8 %collective-permute-start.8 = (bf16[4,2,64,896]{3,2,1,0:T(8,128)(2,1)S(1)}, bf16[4,2,64,896]{3,2,1,0:T(8,128)(2,1)}, u32[]{:S(2)}, u32[]{:S(2)}) collective-permute-start(bf16[4,2,64,896]{3,2,1,0:T(8,128)(2,1)S(1)} %get-tuple-element.97.refs_0_), channel_id=1, source_target_pairs={{0,2},{2,0},{4,6},{6,4},{8,10},{10,8},{12,14},{14,12},{16,18},{18,... | collective-permute-start | bytes 2752520 | tf_op jit(solution)/shard_map/ppermute | solution.py:772
  50.5 32.3 %collective-permute-start.9 = (bf16[4,2,64,896]{3,2,1,0:T(8,128)(2,1)S(1)}, bf16[4,2,64,896]{3,2,1,0:T(8,128)(2,1)}, u32[]{:S(2)}, u32[]{:S(2)}) collective-permute-start(bf16[4,2,64,896]{3,2,1,0:T(8,128)(2,1)S(1)} %get-tuple-element.98.refs_2_), channel_id=1, source_target_pairs={{0,4},{2,6},{4,0},{6,2},{8,12},{10,14},{12,8},{14,10},{16,20},{18,... | collective-permute-start | bytes 2752520 | tf_op jit(solution)/shard_map/ppermute | solution.py:776
  60.5 13.3 %collective-permute-start.5 = (bf16[64,768]{1,0:T(8,128)(2,1)S(1)}, bf16[64,768]{1,0:T(8,128)(2,1)S(1)}, u32[]{:S(2)}, u32[]{:S(2)}) collective-permute-start(bf16[64,768]{1,0:T(8,128)(2,1)S(1)} %maximum_maximum_fusion.refs_0_), channel_id=1, source_target_pairs={{0,8},{2,10},{4,12},{6,14},{8,16},{10,18},{12,20},{14,22},{16,24},... | collective-permute-start | bytes 294920 | tf_op jit(solution)/shard_map/ppermute | solution.py:781
  69.7 11.6 %collective-permute-start.6 = (bf16[64,768]{1,0:T(8,128)(2,1)S(1)}, bf16[64,768]{1,0:T(8,128)(2,1)S(1)}, u32[]{:S(2)}, u32[]{:S(2)}) collective-permute-start(bf16[64,768]{1,0:T(8,128)(2,1)S(1)} %maximum_maximum_fusion.refs_0_), channel_id=1, source_target_pairs={{0,16},{2,18},{4,20},{6,22},{8,24},{10,26},{12,28},{14,30},{16,0},... | collective-permute-start | bytes 294920 | tf_op jit(solution)/shard_map/ppermute | solution.py:781
  69.7 11.6 %collective-permute-start.7 = (bf16[64,768]{1,0:T(8,128)(2,1)S(1)}, bf16[64,768]{1,0:T(8,128)(2,1)S(1)}, u32[]{:S(2)}, u32[]{:S(2)}) collective-permute-start(bf16[64,768]{1,0:T(8,128)(2,1)S(1)} %maximum_maximum_fusion.refs_0_), channel_id=1, source_target_pairs={{0,24},{2,26},{4,28},{6,30},{8,0},{10,2},{12,4},{14,6},{16,8},{18,... | collective-permute-start | bytes 294920 | tf_op jit(solution)/shard_map/ppermute | solution.py:781
  86.7 6.8 %collective-permute-start.10 = (bf16[2,16,64,896]{3,2,1,0:T(8,128)(2,1)}, bf16[2,16,64,896]{3,2,1,0:T(8,128)(2,1)}, u32[]{:S(2)}, u32[]{:S(2)}) collective-permute-start(bf16[2,16,64,896]{3,2,1,0:T(8,128)(2,1)} %bitcast.33.refs_4_.refs_6_.refs_7_), channel_id=1, source_target_pairs={{0,1},{1,0},{2,3},{3,2},{4,5},{5,4},{6,7},{7,6},{8,9},{9,8},{10,11... | collective-permute-start | bytes 11010056 | tf_op jit(solution)/shard_map/ppermute | solution.py:785
  112.5 36.1 %collective-permute-start.11 = (bf16[4,64,768]{2,1,0:T(8,128)(2,1)S(1)}, bf16[4,64,768]{2,1,0:T(8,128)(2,1)S(1)}, u32[]{:S(2)}, u32[]{:S(2)}) collective-permute-start(bf16[4,64,768]{2,1,0:T(8,128)(2,1)S(1)} %gather_z2.1.refs_0_), channel_id=1, source_target_pairs={{0,2},{2,0},{4,6},{6,4},{8,10},{10,8},{12,14},{14,12},{16,18},{18,... | collective-permute-start | bytes 1179656 | tf_op jit(solution)/shard_map/ppermute | solution.py:772
  112.6 36.0 %collective-permute-start.12 = (bf16[4,64,768]{2,1,0:T(8,128)(2,1)S(1)}, bf16[4,64,768]{2,1,0:T(8,128)(2,1)S(1)}, u32[]{:S(2)}, u32[]{:S(2)}) collective-permute-start(bf16[4,64,768]{2,1,0:T(8,128)(2,1)S(1)} %gather_z2.1.refs_0_), channel_id=1, source_target_pairs={{0,4},{2,6},{4,0},{6,2},{8,12},{10,14},{12,8},{14,10},{16,20},{18,... | collective-permute-start | bytes 1179656 | tf_op jit(solution)/shard_map/ppermute | solution.py:776
  114.3 36.3 %collective-permute-start.13 = (bf16[4,64,768]{2,1,0:T(8,128)(2,1)S(1)}, bf16[4,64,768]{2,1,0:T(8,128)(2,1)S(1)}, u32[]{:S(2)}, u32[]{:S(2)}) collective-permute-start(bf16[4,64,768]{2,1,0:T(8,128)(2,1)S(1)} %gather_z2.1.refs_0_), channel_id=1, source_target_pairs={{0,6},{2,4},{4,2},{6,0},{8,14},{10,12},{12,10},{14,8},{16,22},{18,... | collective-permute-start | bytes 1179656 | tf_op jit(solution)/shard_map/ppermute | solution.py:903
  151.4 3.7 collective-permute-start.14
  275.1 20.5 %collective-permute-start.15 = (bf16[4,2,2,384,128]{4,3,2,1,0:T(8,128)(2,1)}, bf16[4,2,2,384,128]{4,3,2,1,0:T(8,128)(2,1)S(1)}, u32[]{:S(2)}, u32[]{:S(2)}) collective-permute-start(bf16[4,2,2,384,128]{4,3,2,1,0:T(8,128)(2,1)} %get-tuple-element.130), channel_id=1, source_target_pairs={{0,1},{1,0},{2,3},{3,2},{4,5},{5,4},{6,7},{7,6},{8,9},{9,8},{10,11... | collective-permute-start | bytes 4718600 | tf_op jit(solution)/shard_map/ppermute | solution.py:785
  297.3 23.6 %collective-permute-start.16 = (bf16[4,384,128]{2,1,0:T(8,128)(2,1)}, bf16[4,384,128]{2,1,0:T(8,128)(2,1)S(1)}, u32[]{:S(2)}, u32[]{:S(2)}) collective-permute-start(bf16[4,384,128]{2,1,0:T(8,128)(2,1)} %get-tuple-element.137), channel_id=1, source_target_pairs={{0,2},{2,0},{4,6},{6,4},{8,10},{10,8},{12,14},{14,12},{16,18},{18,... | collective-permute-start | bytes 1179656 | tf_op jit(solution)/shard_map/ppermute | solution.py:772
  298.8 22.2 %collective-permute-start.17 = (bf16[4,384,128]{2,1,0:T(8,128)(2,1)}, bf16[4,384,128]{2,1,0:T(8,128)(2,1)S(1)}, u32[]{:S(2)}, u32[]{:S(2)}) collective-permute-start(bf16[4,384,128]{2,1,0:T(8,128)(2,1)} %get-tuple-element.138), channel_id=1, source_target_pairs={{0,4},{2,6},{4,0},{6,2},{8,12},{10,14},{12,8},{14,10},{16,20},{18,... | collective-permute-start | bytes 1179656 | tf_op jit(solution)/shard_map/ppermute | solution.py:776
  299.4 21.6 %collective-permute-start.18 = (bf16[4,384,128]{2,1,0:T(8,128)(2,1)S(1)}, bf16[4,384,128]{2,1,0:T(8,128)(2,1)S(1)}, u32[]{:S(2)}, u32[]{:S(2)}) collective-permute-start(bf16[4,384,128]{2,1,0:T(8,128)(2,1)S(1)} %get-tuple-element.139), channel_id=1, source_target_pairs={{0,6},{2,4},{4,2},{6,0},{8,14},{10,12},{12,10},{14,8},{16,22},{18,... | collective-permute-start | bytes 1179656 | tf_op jit(solution)/shard_map/ppermute | solution.py:1123
  335.2 23.7 %collective-permute-start.22 = (bf16[4,2,2,128,128]{4,3,2,1,0:T(8,128)(2,1)}, bf16[4,2,2,128,128]{4,3,2,1,0:T(8,128)(2,1)S(1)}, u32[]{:S(2)}, u32[]{:S(2)}) collective-permute-start(bf16[4,2,2,128,128]{4,3,2,1,0:T(8,128)(2,1)} %get-tuple-element.157), channel_id=1, source_target_pairs={{0,1},{1,0},{2,3},{3,2},{4,5},{5,4},{6,7},{7,6},{8,9},{9,8},{10,11... | collective-permute-start | bytes 1572872 | tf_op jit(solution)/shard_map/ppermute | solution.py:785
  335.3 7.5 %collective-permute-start.19 = (bf16[384,128]{1,0:T(8,128)(2,1)S(1)}, bf16[384,128]{1,0:T(8,128)(2,1)S(1)}, u32[]{:S(2)}, u32[]{:S(2)}) collective-permute-start(bf16[384,128]{1,0:T(8,128)(2,1)S(1)} %get-tuple-element.150), channel_id=1, source_target_pairs={{0,8},{2,10},{4,12},{6,14},{8,16},{10,18},{12,20},{14,22},{16,24},... | collective-permute-start | bytes 294920 | tf_op jit(solution)/shard_map/ppermute | solution.py:781
  335.5 10.7 %collective-permute-start.20 = (bf16[384,128]{1,0:T(8,128)(2,1)S(1)}, bf16[384,128]{1,0:T(8,128)(2,1)S(1)}, u32[]{:S(2)}, u32[]{:S(2)}) collective-permute-start(bf16[384,128]{1,0:T(8,128)(2,1)S(1)} %get-tuple-element.151), channel_id=1, source_target_pairs={{0,16},{2,18},{4,20},{6,22},{8,24},{10,26},{12,28},{14,30},{16,0},... | collective-permute-start | bytes 294920 | tf_op jit(solution)/shard_map/ppermute | solution.py:781
  337.3 8.9 %collective-permute-start.21 = (bf16[384,128]{1,0:T(8,128)(2,1)S(1)}, bf16[384,128]{1,0:T(8,128)(2,1)S(1)}, u32[]{:S(2)}, u32[]{:S(2)}) collective-permute-start(bf16[384,128]{1,0:T(8,128)(2,1)S(1)} %get-tuple-element.152), channel_id=1, source_target_pairs={{0,24},{2,26},{4,28},{6,30},{8,0},{10,2},{12,4},{14,6},{16,8},{18,... | collective-permute-start | bytes 294920 | tf_op jit(solution)/shard_map/ppermute | solution.py:781
  359.6 6.2 %collective-permute-start.23 = (bf16[4,128,128]{2,1,0:T(8,128)(2,1)S(1)}, bf16[4,128,128]{2,1,0:T(8,128)(2,1)S(1)}, u32[]{:S(2)}, u32[]{:S(2)}) collective-permute-start(bf16[4,128,128]{2,1,0:T(8,128)(2,1)S(1)} %get-tuple-element.160), channel_id=1, source_target_pairs={{0,2},{2,0},{4,6},{6,4},{8,10},{10,8},{12,14},{14,12},{16,18},{18,... | collective-permute-start | bytes 393224 | tf_op jit(solution)/shard_map/ppermute | solution.py:772
  361.0 6.9 %collective-permute-start.24 = (bf16[4,128,128]{2,1,0:T(8,128)(2,1)S(1)}, bf16[4,128,128]{2,1,0:T(8,128)(2,1)S(1)}, u32[]{:S(2)}, u32[]{:S(2)}) collective-permute-start(bf16[4,128,128]{2,1,0:T(8,128)(2,1)S(1)} %get-tuple-element.161), channel_id=1, source_target_pairs={{0,4},{2,6},{4,0},{6,2},{8,12},{10,14},{12,8},{14,10},{16,20},{18,... | collective-permute-start | bytes 393224 | tf_op jit(solution)/shard_map/ppermute | solution.py:776
  361.7 6.3 %collective-permute-start.25 = (bf16[4,128,128]{2,1,0:T(8,128)(2,1)S(1)}, bf16[4,128,128]{2,1,0:T(8,128)(2,1)S(1)}, u32[]{:S(2)}, u32[]{:S(2)}) collective-permute-start(bf16[4,128,128]{2,1,0:T(8,128)(2,1)S(1)} %get-tuple-element.162), channel_id=1, source_target_pairs={{0,6},{2,4},{4,2},{6,0},{8,14},{10,12},{12,10},{14,8},{16,22},{18,... | collective-permute-start | bytes 393224 | tf_op jit(solution)/shard_map/ppermute | solution.py:1123
  368.6 18.0 %collective-permute-start.26 = (bf16[128,128]{1,0:T(8,128)(2,1)S(1)}, bf16[128,128]{1,0:T(8,128)(2,1)S(1)}, u32[]{:S(2)}, u32[]{:S(2)}) collective-permute-start(bf16[128,128]{1,0:T(8,128)(2,1)S(1)} %get-tuple-element.164), channel_id=1, source_target_pairs={{0,8},{2,10},{4,12},{6,14},{8,16},{10,18},{12,20},{14,22},{16,24},... | collective-permute-start | bytes 98312 | tf_op jit(solution)/shard_map/ppermute | solution.py:781
  371.3 15.3 %collective-permute-start.27 = (bf16[128,128]{1,0:T(8,128)(2,1)S(1)}, bf16[128,128]{1,0:T(8,128)(2,1)S(1)}, u32[]{:S(2)}, u32[]{:S(2)}) collective-permute-start(bf16[128,128]{1,0:T(8,128)(2,1)S(1)} %get-tuple-element.165), channel_id=1, source_target_pairs={{0,16},{2,18},{4,20},{6,22},{8,24},{10,26},{12,28},{14,30},{16,0},... | collective-permute-start | bytes 98312 | tf_op jit(solution)/shard_map/ppermute | solution.py:781
  373.0 13.5 %collective-permute-start.28 = (bf16[128,128]{1,0:T(8,128)(2,1)S(1)}, bf16[128,128]{1,0:T(8,128)(2,1)S(1)}, u32[]{:S(2)}, u32[]{:S(2)}) collective-permute-start(bf16[128,128]{1,0:T(8,128)(2,1)S(1)} %get-tuple-element.166), channel_id=1, source_target_pairs={{0,24},{2,26},{4,28},{6,30},{8,0},{10,2},{12,4},{14,6},{16,8},{18,... | collective-permute-start | bytes 98312 | tf_op jit(solution)/shard_map/ppermute | solution.py:781
  (32 other events, 370.8 us)
Sparse Core Ops, SparseCore 0:
  34.0 149.3 all-gather.2

commit v2 on v0

--- a/solution.py
+++ b/solution.py
@@ -969,6 +969,8 @@
         one.send_rest()
         one.parts[0] = after(one.parts[0], *others)
         one.join_rest()
+        two.shard = after(two.shard, one.own)
+        two.send_z()
         lanes = pl.ds(3 * self.column // 2, STACK)
         moves = [
             m
@@ -985,9 +987,6 @@
         return one.sources, self.places, one.sources, moves
 
     def after_qkv(self, q):
-        two = self.piece2
-        two.shard = after(two.shard, q)
-        two.send_z()
         return q
 
     def between_images(self, o):

time: 399 us -> 408 us (1.023)
  waiting for transfers between devices: 56.5 us -> 66.6 us
    ppermute x1, waiting for transfers between devices: 1.13 us -> 13.1 us  [send_layer(): diagonal = lax.ppermute(self.a, 'fsdp', [(f, f ^ 3) for f in range(16)])]
    ppermute x4, waiting for transfers between devices: 8.99 us -> 3.4 us  [other_core(): return lax.ppermute(array, 'tensor', [(0, 1), (1, 0)])]
  transfers between devices with their start and end apart: 30 -> 30, of which waited for: 14 -> 15; matrix products, arithmetic and copies ran while one was open for 1% -> 1% of each run, Pallas kernels for 38% -> 37%
where the time goes in v2:
time: 408 us; the launch traced here: 402 us
  Pallas kernels  261 us (64%)
  waiting for transfers between devices  66.6 us (16%)
  starting transfers between devices  45.9 us (11%)
  between operations  15.1 us (4%)
  local copies, waits for them, and re-layouts  11.7 us (3%)
    pallas_call x1, Pallas kernels, mlp(): pl.pallas_call(partial(mlp_kernel, len(up1)), grid=(tiles, images), in_sp...  76.7 us
    pallas_call x2, Pallas kernels, per_image(): pl.pallas_call(kernel, grid=(HEADS // 2,), in_specs=in_specs, out_specs=o...  36.5 us
    pallas_call x2, Pallas kernels, per_image(): pl.pallas_call(into(kernel, count), grid=(HEADS // 2,), in_specs=in_specs...  36.4 us
    ppermute x12, starting transfers between devices, along_z(): return lax.ppermute(array, 'fsdp', pairs)  29.5 us
    pallas_call x2, Pallas kernels, qkv_back(): pl.pallas_call(partial(qkv_back_kernel, len(sources), image), grid=(1,),...  23.9 us
    pallas_call x8, Pallas kernels, move(): pl.pallas_call(kernel, in_specs=[smem()] + [any_space()] * len(parts), ou...  20.1 us
    ppermute x5, waiting for transfers between devices, along_x(): return lax.ppermute(array, 'fsdp', [(f, f ^ 1) for f in range(16)])  19.6 us
    pallas_call x1, Pallas kernels, qkv_project(): pl.pallas_call(partial(qkv_kernel, len(sources), moves), grid_spec=grid_s...  18.9 us
  transfers between devices with their start and end apart: 30, of which 15 were waited for; matrix products, arithmetic and copies ran while one was open for 1% of the time, Pallas kernels for 37%

profile of v2, /device:TPU:0, one launch (start us, length us, event | category | flops | bytes accessed | tf_op | source)
XLA Modules:
  0.0 401.7 jit_solution(3414584672071121996)
XLA Ops:
  10.1 3.1 collective-permute-start
  21.9 9.0 %collective-permute-done.1.refs_2_ = bf16[64,1792]{1,0:T(8,128)(2,1)} collective-permute-done((bf16[64,1792]{1,0:T(8,128)(2,1)S(1)}, bf16[64,1792]{1,0:T(8,128)(2,1)}, u32[]{:S(2)}, u32[]{:S(2)}) %collective-permute-start.1) | collective-permute-done | bytes 229408 | tf_op jit(solution)/shard_map/ppermute | solution.py:781
  30.9 2.9 gather_z1.1
  37.0 5.2 %untangle.2.refs_3_.tokens_ref.refs_1_ = bf16[2,577,1024]{2,1,0:T(8,128)(2,1)S(1)} custom-call(bf16[577,2,1024]{2,1,0:T(2,128)(2,1)S(1)} %bitcast.82), custom_call_target="tpu_custom_call" | custom-call | tf_op jit(solution)/shard_map/untangle/pallas_call | solution.py:111
  43.6 2.9 collective-permute-done.3.refs_1_
  53.4 5.2 %untangle.3.refs_3_ = bf16[2,577,1024]{2,1,0:T(8,128)(2,1)S(1)} custom-call(bf16[577,2,1024]{2,1,0:T(2,128)(2,1)S(1)} %bitcast.83), custom_call_target="tpu_custom_call" | custom-call | tf_op jit(solution)/shard_map/untangle/pallas_call | solution.py:111
  60.6 15.1 %collective-permute-done.5.refs_1_ = bf16[4,2,64,896]{3,2,1,0:T(8,128)(2,1)S(1)} collective-permute-done((bf16[4,2,64,896]{3,2,1,0:T(8,128)(2,1)S(1)}, bf16[4,2,64,896]{3,2,1,0:T(8,128)(2,1)S(1)}, u32[]{:S(2)}, u32[]{:S(2)}) %collective-permute-start.5) | collective-permute-done | bytes 917536 | tf_op jit(solution)/shard_map/ppermute | solution.py:772
  76.3 3.8 gather_xy1.1
  81.4 6.2 %collective-permute-start.10 = (bf16[64,768]{1,0:T(8,128)(2,1)S(1)}, bf16[64,768]{1,0:T(8,128)(2,1)S(1)}, u32[]{:S(2)}, u32[]{:S(2)}) collective-permute-start(bf16[64,768]{1,0:T(8,128)(2,1)S(1)} %maximum_maximum_fusion.refs_0_), channel_id=1, source_target_pairs={{0,24},{2,26},{4,28},{6,30},{8,0},{10,2},{12,4},{14,6},{16,8},{18,... | collective-permute-start | bytes 294920 | tf_op jit(solution)/shard_map/ppermute | solution.py:781
  87.6 4.9 %collective-permute-start.8 = (bf16[64,768]{1,0:T(8,128)(2,1)S(1)}, bf16[64,768]{1,0:T(8,128)(2,1)S(1)}, u32[]{:S(2)}, u32[]{:S(2)}) collective-permute-start(bf16[64,768]{1,0:T(8,128)(2,1)S(1)} %maximum_maximum_fusion.refs_0_), channel_id=1, source_target_pairs={{0,8},{2,10},{4,12},{6,14},{8,16},{10,18},{12,20},{14,22},{16,24},... | collective-permute-start | bytes 294920 | tf_op jit(solution)/shard_map/ppermute | solution.py:781
  93.9 18.9 %qkv_project.1 = (bf16[2,577,1024]{2,1,0:T(8,128)(2,1)}, bf16[2,577,1024]{2,1,0:T(8,128)(2,1)}, bf16[2,577,1024]{2,1,0:T(8,128)(2,1)}, bf16[2,577,128]{2,1,0:T(8...) custom-call(s32[4]{0:T(128)} %pad_add_fusion.1.refs_0_, s32[10]{0:T(128)} %stack.97.places_ref.refs_1_.p, ...), custom_call_target="tpu_custom_call" | custom-call | flops 7260340224 | bytes 20971520 | tf_op jit(solution)/shard_map/qkv_project/pallas_call | solution.py:268
  112.8 16.3 %attend.2 = (bf16[2,577,1024]{2,1,0:T(8,128)(2,1)}, bf16[32,577,577]{2,1,0:T(8,128)(2,1)}, f32[2,577,1024]{2,1,0:T(8,128)}) custom-call(bf16[2,577,1024]{2,1,0:T(8,128)(2,1)} %get-tuple-element.100.q_ref.refs_0_, bf16[2,577,1024]{2,1,0:T(8,128)(2,1)} %get-tuple-element.101.k_ref.refs_1_, bf16[2,577,1024]{2,1,0:T(8,128)(2,1)} %get-tuple-element.102.v_ref.refs_2_), custom_call_target="tpu_custom_call" | custom-call | flops 5454708736 | bytes 20971520 | tf_op jit(solution)/shard_map/attend/pallas_call | solution.py:318
  133.8 16.3 %attend.3 = (bf16[2,577,1024]{2,1,0:T(8,128)(2,1)}, bf16[32,577,577]{2,1,0:T(8,128)(2,1)}, f32[2,577,1024]{2,1,0:T(8,128)}) custom-call(bf16[2,577,1024]{2,1,0:T(8,128)(2,1)} %get-tuple-element.100.q_ref.refs_0_, bf16[2,577,1024]{2,1,0:T(8,128)(2,1)} %get-tuple-element.101.k_ref.refs_1_, ...), custom_call_target="tpu_custom_call", output_to_operand_aliasing={{0}: (3, {}), {1}: (4, {}), {2}: (5, {})} | custom-call | flops 5454708736 | bytes 20971520 | tf_op jit(solution)/shard_map/attend/pallas_call | solution.py:322
  150.7 3.2 collective-permute-done.12.refs_2_
  153.9 13.1 %collective-permute-done.13.refs_3_ = bf16[4,64,768]{2,1,0:T(8,128)(2,1)S(1)} collective-permute-done((bf16[4,64,768]{2,1,0:T(8,128)(2,1)S(1)}, bf16[4,64,768]{2,1,0:T(8,128)(2,1)S(1)}, u32[]{:S(2)}, u32[]{:S(2)}) %collective-permute-start.13) | collective-permute-done | bytes 393248 | tf_op jit(solution)/shard_map/ppermute | solution.py:903
  167.9 3.4 collective-permute-done.14.refs_1_.refs_6_.refs_7_
  172.5 3.0 stacks2.1
  175.6 10.7 %out_project.1 = (f32[2,577,1024]{2,1,0:T(8,128)}, bf16[2,577,128]{2,1,0:T(8,128)(2,1)}) custom-call(s32[4]{0:T(128)} %pad_add_fusion.1.refs_0_, s32[2,2]{1,0:T(2,128)} %constant_dynamic-slice_fusion.refs_2_.refs_1_.refs_0_.index_ref, s32[2,2]{1,0:T(2,128)} %constant_dynamic-slice_fusion.refs_2_.refs_1_.refs_0_.index_ref, bf16[2,577,1024]{2,1,0:T(8,128)(2,1)} %copy-done, ...), custom_call_target="tpu_custom_call" | custom-call | flops 2420113408 | bytes 12582912 | tf_op jit(solution)/shard_map/out_project/pallas_call | solution.py:402
  186.3 3.7 all-gather.3.cloned.1.call-done
  190.0 76.7 %mlp.1 = (bf16[577,2,1024]{2,1,0:T(2,128)(2,1)}, f32[2,577,1024]{2,1,0:T(8,128)}, bf16[1024,128]{1,0:T(8,128)(2,1)}, bf16[4096,128]{1,0:T(8,128)(2,1)}, bf16[409...) custom-call(s32[2,2]{1,0:T(2,128)} %constant_dynamic-slice_fusion.refs_2_.refs_1_.refs_0_.index_ref, ...), custom_call_target="tpu_custom_call" | custom-call | flops 38721814528 | bytes 41943040 | tf_op jit(solution)/shard_map/mlp/pallas_call | solution.py:589
  266.7 10.6 %out_back.1 = (bf16[2,577,1024]{2,1,0:T(8,128)(2,1)}, bf16[1024,128]{1,0:T(8,128)(2,1)}, bf16[1024,128]{1,0:T(8,128)(2,1)}) custom-call(s32[4]{0:T(128)} %pad_add_fusion.1.refs_0_, s32[2,2]{1,0:T(2,128)} %constant_dynamic-slice_fusion.refs_2_.refs_1_.refs_0_.index_ref, s32[2,2]{1,0:T(2,128)} %constant_dynamic-slice_fusion.refs_2_.refs_1_.refs_0_.index_ref, ...), custom_call_target="tpu_custom_call" | custom-call | flops 2420113408 | bytes 12582912 | tf_op jit(solution)/shard_map/out_back/pallas_call | solution.py:457
  277.3 4.4 %scatter_core1.1 = (bf16[4,2,2,384,128]{4,3,2,1,0:T(8,128)(2,1)}, bf16[4,2,2,384,128]{4,3,2,1,0:T(8,128)(2,1)}) custom-call(s32[10]{0:T(128)} %stack.97.places_ref.refs_1_.p, bf16[4,2,2,2,32,128]{5,4,3,2,1,0:T(8,128)(2,1)} %bitcast.103, bf16[4,2,2,2,32,128]{5,4,3,2,1,0:T(8,128)(2,1)} %bitcast.102, bf16[4,2,2,2,32,128]{5,4,3,2,1,0:T(8,128)(2,1)} %bitcast.101, ...), custom_call_target="tpu_custom_call" | custom-call | tf_op jit(solution)/shard_map/scatter_core1/pallas_call | solution.py:814
  282.0 20.2 %attend_back.2 = (bf16[2,577,1024]{2,1,0:T(8,128)(2,1)}, bf16[2,577,1024]{2,1,0:T(8,128)(2,1)}, bf16[2,577,1024]{2,1,0:T(8,128)(2,1)}) custom-call(bf16[2,577,1024]{2,1,0:T(8,128)(2,1)} %get-tuple-element.100.q_ref.refs_0_, bf16[2,577,1024]{2,1,0:T(8,128)(2,1)} %get-tuple-element.101.k_ref.refs_1_, bf16[2,577,1024]{2,1,0:T(8,128)(2,1)} %get-tuple-element.102.v_ref.refs_2_, ...), custom_call_target="tpu_custom_call" | custom-call | flops 10909417472 | bytes 25165824 | tf_op jit(solution)/shard_map/attend_back/pallas_call | solution.py:318
  307.5 20.1 %attend_back.3 = (bf16[2,577,1024]{2,1,0:T(8,128)(2,1)}, bf16[2,577,1024]{2,1,0:T(8,128)(2,1)}, bf16[2,577,1024]{2,1,0:T(8,128)(2,1)}) custom-call(bf16[2,577,1024]{2,1,0:T(8,128)(2,1)} %get-tuple-element.100.q_ref.refs_0_, bf16[2,577,1024]{2,1,0:T(8,128)(2,1)} %get-tuple-element.101.k_ref.refs_1_, ...), custom_call_target="tpu_custom_call", output_to_operand_aliasing={{0}: (7, {}), {1}: (8, {}), {2}: (9, {})} | custom-call | flops 10909417472 | bytes 25165824 | tf_op jit(solution)/shard_map/attend_back/pallas_call | solution.py:322
  328.4 10.4 %qkv_grads.1 = (bf16[2,577,128]{2,1,0:T(8,128)(2,1)}, bf16[3072,128]{1,0:T(8,128)(2,1)}, bf16[1024,128]{1,0:T(8,128)(2,1)}) custom-call(s32[2,2]{1,0:T(2,128)} %constant_dynamic-slice_fusion.refs_2_.refs_1_.refs_0_.index_ref, bf16[2,577,1024]{2,1,0:T(8,128)(2,1)} %copy-done, bf16[2,577,1024]{2,1,0:T(8,128)(2,1)} %get-tuple-element.145.dq_ref.refs_3_, ...), custom_call_target="tpu_custom_call" | custom-call | flops 2420113408 | bytes 12582912 | tf_op jit(solution)/shard_map/qkv_grads/pallas_call | solution.py:674
  338.8 3.0 scatter_core2.1
  343.5 3.0 collective-permute-start.21
  346.5 2.9 collective-permute-done.19.first
  349.4 3.4 collective-permute-done.20.second
  354.3 11.3 %qkv_back.2.refs_11_ = f32[577,1024]{1,0:T(8,128)} custom-call(s32[4]{0:T(128)} %pad_add_fusion.1.refs_0_, bf16[2,577,1024]{2,1,0:T(8,128)(2,1)} %copy-done, f32[2,577,1024]{2,1,0:T(8,128)} %get-tuple-element.119.refs_3_.refs_2_, bf16[2,577,1024]{2,1,0:T(8,128)(2,1)} %get-tuple-element.145.dq_ref.refs_3_, ...), custom_call_target="tpu_custom_call" | custom-call | flops 3630170112 | bytes 18874368 | tf_op jit(solution)/shard_map/qkv_back/pallas_call | solution.py:744
  369.8 2.7 collective-permute-done.23.two
  380.6 12.6 %qkv_back.3 = f32[577,2,1024]{2,1,0:T(2,128)} custom-call(s32[4]{0:T(128)} %pad_add_fusion.1.refs_0_, bf16[2,577,1024]{2,1,0:T(8,128)(2,1)} %copy-done, f32[2,577,1024]{2,1,0:T(8,128)} %get-tuple-element.119.refs_3_.refs_2_, bf16[2,577,1024]{2,1,0:T(8,128)(2,1)} %get-tuple-element.145.dq_ref.refs_3_, ...), custom_call_target="tpu_custom_call" | custom-call | flops 3630170112 | bytes 18874368 | tf_op jit(solution)/shard_map/qkv_back/pallas_call | solution.py:744
  (162 shorter events, 58.3 us)
Async XLA Ops:
  7.2 182.7 %all-gather.3.cloned.1.call-start = ((), (), s32[]{:S(2)}) async-start(), calls=%async_computation | async-start | bytes 19464192 | tf_op jit(solution)/shard_map/all_gather | solution.py:965
  8.6 28.4 %copy-start.3 = (bf16[2,577,1024]{2,0,1:T(2,128)(2,1)S(1)}, bf16[2,577,1024]{2,0,1:T(2,128)(2,1)}, u32[]{:S(2)}) copy-start(bf16[2,577,1024]{2,0,1:T(2,128)(2,1)} %param.24) | copy-start | bytes 7090180
  10.1 11.8 %collective-permute-start = (bf16[64,1792]{1,0:T(8,128)(2,1)S(1)}, bf16[64,1792]{1,0:T(8,128)(2,1)}, u32[]{:S(2)}, u32[]{:S(2)}) collective-permute-start(bf16[64,1792]{1,0:T(8,128)(2,1)S(1)} %fusion.2.refs_0_), channel_id=1, source_target_pairs={{0,8},{2,10},{4,12},{6,14},{8,16},{10,18},{12,20},{14,22},{16,24},... | collective-permute-start | bytes 688136 | tf_op jit(solution)/shard_map/ppermute | solution.py:781
  13.2 17.7 %collective-permute-start.1 = (bf16[64,1792]{1,0:T(8,128)(2,1)S(1)}, bf16[64,1792]{1,0:T(8,128)(2,1)}, u32[]{:S(2)}, u32[]{:S(2)}) collective-permute-start(bf16[64,1792]{1,0:T(8,128)(2,1)S(1)} %fusion.2.refs_0_), channel_id=1, source_target_pairs={{0,16},{2,18},{4,20},{6,22},{8,24},{10,26},{12,28},{14,30},{16,0},... | collective-permute-start | bytes 688136 | tf_op jit(solution)/shard_map/ppermute | solution.py:781
  15.8 15.1 %collective-permute-start.2 = (bf16[64,1792]{1,0:T(8,128)(2,1)S(1)}, bf16[64,1792]{1,0:T(8,128)(2,1)}, u32[]{:S(2)}, u32[]{:S(2)}) collective-permute-start(bf16[64,1792]{1,0:T(8,128)(2,1)S(1)} %fusion.2.refs_0_), channel_id=1, source_target_pairs={{0,24},{2,26},{4,28},{6,30},{8,0},{10,2},{12,4},{14,6},{16,8},{18,... | collective-permute-start | bytes 688136 | tf_op jit(solution)/shard_map/ppermute | solution.py:781
  33.9 12.6 %collective-permute-start.3 = (bf16[4,64,896]{2,1,0:T(8,128)(2,1)}, bf16[4,64,896]{2,1,0:T(8,128)(2,1)S(1)}, u32[]{:S(2)}, u32[]{:S(2)}) collective-permute-start(bf16[4,64,896]{2,1,0:T(8,128)(2,1)} %get-tuple-element.95.refs_0_), channel_id=1, source_target_pairs={{0,4},{2,6},{4,0},{6,2},{8,12},{10,14},{12,8},{14,10},{16,20},{18,... | collective-permute-start | bytes 1376264 | tf_op jit(solution)/shard_map/ppermute | solution.py:776
  35.5 12.3 %collective-permute-start.4 = (bf16[4,64,896]{2,1,0:T(8,128)(2,1)}, bf16[4,64,896]{2,1,0:T(8,128)(2,1)S(1)}, u32[]{:S(2)}, u32[]{:S(2)}) collective-permute-start(bf16[4,64,896]{2,1,0:T(8,128)(2,1)} %get-tuple-element.96.refs_2_), channel_id=1, source_target_pairs={{0,2},{2,0},{4,6},{6,4},{8,10},{10,8},{12,14},{14,12},{16,18},{18,... | collective-permute-start | bytes 1376264 | tf_op jit(solution)/shard_map/ppermute | solution.py:772
  48.9 26.9 %collective-permute-start.5 = (bf16[4,2,64,896]{3,2,1,0:T(8,128)(2,1)S(1)}, bf16[4,2,64,896]{3,2,1,0:T(8,128)(2,1)S(1)}, u32[]{:S(2)}, u32[]{:S(2)}) collective-permute-start(bf16[4,2,64,896]{3,2,1,0:T(8,128)(2,1)S(1)} %get-tuple-element.98.refs_0_), channel_id=1, source_target_pairs={{0,2},{2,0},{4,6},{6,4},{8,10},{10,8},{12,14},{14,12},{16,18},{18,... | collective-permute-start | bytes 2752520 | tf_op jit(solution)/shard_map/ppermute | solution.py:772
  50.4 25.9 %collective-permute-start.6 = (bf16[4,2,64,896]{3,2,1,0:T(8,128)(2,1)S(1)}, bf16[4,2,64,896]{3,2,1,0:T(8,128)(2,1)}, u32[]{:S(2)}, u32[]{:S(2)}) collective-permute-start(bf16[4,2,64,896]{3,2,1,0:T(8,128)(2,1)S(1)} %get-tuple-element.99.refs_2_), channel_id=1, source_target_pairs={{0,4},{2,6},{4,0},{6,2},{8,12},{10,14},{12,8},{14,10},{16,20},{18,... | collective-permute-start | bytes 2752520 | tf_op jit(solution)/shard_map/ppermute | solution.py:776
  80.1 13.7 %collective-permute-start.7 = (bf16[2,16,64,896]{3,2,1,0:T(8,128)(2,1)}, bf16[2,16,64,896]{3,2,1,0:T(8,128)(2,1)}, u32[]{:S(2)}, u32[]{:S(2)}) collective-permute-start(bf16[2,16,64,896]{3,2,1,0:T(8,128)(2,1)} %bitcast.22.refs_4_.refs_6_.refs_7_), channel_id=1, source_target_pairs={{0,1},{1,0},{2,3},{3,2},{4,5},{5,4},{6,7},{7,6},{8,9},{9,8},{10,11... | collective-permute-start | bytes 11010056 | tf_op jit(solution)/shard_map/ppermute | solution.py:785
  81.4 47.7 %collective-permute-start.10 = (bf16[64,768]{1,0:T(8,128)(2,1)S(1)}, bf16[64,768]{1,0:T(8,128)(2,1)S(1)}, u32[]{:S(2)}, u32[]{:S(2)}) collective-permute-start(bf16[64,768]{1,0:T(8,128)(2,1)S(1)} %maximum_maximum_fusion.refs_0_), channel_id=1, source_target_pairs={{0,24},{2,26},{4,28},{6,30},{8,0},{10,2},{12,4},{14,6},{16,8},{18,... | collective-permute-start | bytes 294920 | tf_op jit(solution)/shard_map/ppermute | solution.py:781
  87.6 41.5 %collective-permute-start.8 = (bf16[64,768]{1,0:T(8,128)(2,1)S(1)}, bf16[64,768]{1,0:T(8,128)(2,1)S(1)}, u32[]{:S(2)}, u32[]{:S(2)}) collective-permute-start(bf16[64,768]{1,0:T(8,128)(2,1)S(1)} %maximum_maximum_fusion.refs_0_), channel_id=1, source_target_pairs={{0,8},{2,10},{4,12},{6,14},{8,16},{10,18},{12,20},{14,22},{16,24},... | collective-permute-start | bytes 294920 | tf_op jit(solution)/shard_map/ppermute | solution.py:781
  92.5 36.6 %collective-permute-start.9 = (bf16[64,768]{1,0:T(8,128)(2,1)S(1)}, bf16[64,768]{1,0:T(8,128)(2,1)S(1)}, u32[]{:S(2)}, u32[]{:S(2)}) collective-permute-start(bf16[64,768]{1,0:T(8,128)(2,1)S(1)} %maximum_maximum_fusion.refs_0_), channel_id=1, source_target_pairs={{0,16},{2,18},{4,20},{6,22},{8,24},{10,26},{12,28},{14,30},{16,0},... | collective-permute-start | bytes 294920 | tf_op jit(solution)/shard_map/ppermute | solution.py:781
  130.2 20.4 %collective-permute-start.11 = (bf16[4,64,768]{2,1,0:T(8,128)(2,1)S(1)}, bf16[4,64,768]{2,1,0:T(8,128)(2,1)S(1)}, u32[]{:S(2)}, u32[]{:S(2)}) collective-permute-start(bf16[4,64,768]{2,1,0:T(8,128)(2,1)S(1)} %gather_z2.1.refs_0_), channel_id=1, source_target_pairs={{0,2},{2,0},{4,6},{6,4},{8,10},{10,8},{12,14},{14,12},{16,18},{18,... | collective-permute-start | bytes 1179656 | tf_op jit(solution)/shard_map/ppermute | solution.py:772
  131.9 22.0 %collective-permute-start.12 = (bf16[4,64,768]{2,1,0:T(8,128)(2,1)S(1)}, bf16[4,64,768]{2,1,0:T(8,128)(2,1)S(1)}, u32[]{:S(2)}, u32[]{:S(2)}) collective-permute-start(bf16[4,64,768]{2,1,0:T(8,128)(2,1)S(1)} %gather_z2.1.refs_0_), channel_id=1, source_target_pairs={{0,4},{2,6},{4,0},{6,2},{8,12},{10,14},{12,8},{14,10},{16,20},{18,... | collective-permute-start | bytes 1179656 | tf_op jit(solution)/shard_map/ppermute | solution.py:776
  131.9 35.1 %collective-permute-start.13 = (bf16[4,64,768]{2,1,0:T(8,128)(2,1)S(1)}, bf16[4,64,768]{2,1,0:T(8,128)(2,1)S(1)}, u32[]{:S(2)}, u32[]{:S(2)}) collective-permute-start(bf16[4,64,768]{2,1,0:T(8,128)(2,1)S(1)} %gather_z2.1.refs_0_), channel_id=1, source_target_pairs={{0,6},{2,4},{4,2},{6,0},{8,14},{10,12},{12,10},{14,8},{16,22},{18,... | collective-permute-start | bytes 1179656 | tf_op jit(solution)/shard_map/ppermute | solution.py:903
  167.8 3.5 collective-permute-start.14
  281.7 20.6 %collective-permute-start.15 = (bf16[4,2,2,384,128]{4,3,2,1,0:T(8,128)(2,1)}, bf16[4,2,2,384,128]{4,3,2,1,0:T(8,128)(2,1)S(1)}, u32[]{:S(2)}, u32[]{:S(2)}) collective-permute-start(bf16[4,2,2,384,128]{4,3,2,1,0:T(8,128)(2,1)} %get-tuple-element.134), channel_id=1, source_target_pairs={{0,1},{1,0},{2,3},{3,2},{4,5},{5,4},{6,7},{7,6},{8,9},{9,8},{10,11... | collective-permute-start | bytes 4718600 | tf_op jit(solution)/shard_map/ppermute | solution.py:785
  304.0 23.6 %collective-permute-start.16 = (bf16[4,384,128]{2,1,0:T(8,128)(2,1)}, bf16[4,384,128]{2,1,0:T(8,128)(2,1)S(1)}, u32[]{:S(2)}, u32[]{:S(2)}) collective-permute-start(bf16[4,384,128]{2,1,0:T(8,128)(2,1)} %get-tuple-element.141), channel_id=1, source_target_pairs={{0,2},{2,0},{4,6},{6,4},{8,10},{10,8},{12,14},{14,12},{16,18},{18,... | collective-permute-start | bytes 1179656 | tf_op jit(solution)/shard_map/ppermute | solution.py:772
  305.4 22.2 %collective-permute-start.17 = (bf16[4,384,128]{2,1,0:T(8,128)(2,1)}, bf16[4,384,128]{2,1,0:T(8,128)(2,1)S(1)}, u32[]{:S(2)}, u32[]{:S(2)}) collective-permute-start(bf16[4,384,128]{2,1,0:T(8,128)(2,1)} %get-tuple-element.142), channel_id=1, source_target_pairs={{0,4},{2,6},{4,0},{6,2},{8,12},{10,14},{12,8},{14,10},{16,20},{18,... | collective-permute-start | bytes 1179656 | tf_op jit(solution)/shard_map/ppermute | solution.py:776
  306.0 21.6 %collective-permute-start.18 = (bf16[4,384,128]{2,1,0:T(8,128)(2,1)S(1)}, bf16[4,384,128]{2,1,0:T(8,128)(2,1)S(1)}, u32[]{:S(2)}, u32[]{:S(2)}) collective-permute-start(bf16[4,384,128]{2,1,0:T(8,128)(2,1)S(1)} %get-tuple-element.143), channel_id=1, source_target_pairs={{0,6},{2,4},{4,2},{6,0},{8,14},{10,12},{12,10},{14,8},{16,22},{18,... | collective-permute-start | bytes 1179656 | tf_op jit(solution)/shard_map/ppermute | solution.py:1124
  328.4 24.5 %copy-start.12 = (s32[10]{0:T(128)S(1)}, s32[10]{0:T(128)}, u32[]{:S(2)}) copy-start(s32[10]{0:T(128)} %stack.97.places_ref.refs_1_.p) | copy-start | bytes 124
  341.8 23.7 %collective-permute-start.22 = (bf16[4,2,2,128,128]{4,3,2,1,0:T(8,128)(2,1)}, bf16[4,2,2,128,128]{4,3,2,1,0:T(8,128)(2,1)S(1)}, u32[]{:S(2)}, u32[]{:S(2)}) collective-permute-start(bf16[4,2,2,128,128]{4,3,2,1,0:T(8,128)(2,1)} %get-tuple-element.161), channel_id=1, source_target_pairs={{0,1},{1,0},{2,3},{3,2},{4,5},{5,4},{6,7},{7,6},{8,9},{9,8},{10,11... | collective-permute-start | bytes 1572872 | tf_op jit(solution)/shard_map/ppermute | solution.py:785
  341.9 7.5 %collective-permute-start.19 = (bf16[384,128]{1,0:T(8,128)(2,1)S(1)}, bf16[384,128]{1,0:T(8,128)(2,1)S(1)}, u32[]{:S(2)}, u32[]{:S(2)}) collective-permute-start(bf16[384,128]{1,0:T(8,128)(2,1)S(1)} %get-tuple-element.154), channel_id=1, source_target_pairs={{0,8},{2,10},{4,12},{6,14},{8,16},{10,18},{12,20},{14,22},{16,24},... | collective-permute-start | bytes 294920 | tf_op jit(solution)/shard_map/ppermute | solution.py:781
  342.1 10.7 %collective-permute-start.20 = (bf16[384,128]{1,0:T(8,128)(2,1)S(1)}, bf16[384,128]{1,0:T(8,128)(2,1)S(1)}, u32[]{:S(2)}, u32[]{:S(2)}) collective-permute-start(bf16[384,128]{1,0:T(8,128)(2,1)S(1)} %get-tuple-element.155), channel_id=1, source_target_pairs={{0,16},{2,18},{4,20},{6,22},{8,24},{10,26},{12,28},{14,30},{16,0},... | collective-permute-start | bytes 294920 | tf_op jit(solution)/shard_map/ppermute | solution.py:781
  343.5 9.3 %collective-permute-start.21 = (bf16[384,128]{1,0:T(8,128)(2,1)S(1)}, bf16[384,128]{1,0:T(8,128)(2,1)S(1)}, u32[]{:S(2)}, u32[]{:S(2)}) collective-permute-start(bf16[384,128]{1,0:T(8,128)(2,1)S(1)} %get-tuple-element.156), channel_id=1, source_target_pairs={{0,24},{2,26},{4,28},{6,30},{8,0},{10,2},{12,4},{14,6},{16,8},{18,... | collective-permute-start | bytes 294920 | tf_op jit(solution)/shard_map/ppermute | solution.py:781
  366.2 6.2 %collective-permute-start.23 = (bf16[4,128,128]{2,1,0:T(8,128)(2,1)S(1)}, bf16[4,128,128]{2,1,0:T(8,128)(2,1)S(1)}, u32[]{:S(2)}, u32[]{:S(2)}) collective-permute-start(bf16[4,128,128]{2,1,0:T(8,128)(2,1)S(1)} %get-tuple-element.164), channel_id=1, source_target_pairs={{0,2},{2,0},{4,6},{6,4},{8,10},{10,8},{12,14},{14,12},{16,18},{18,... | collective-permute-start | bytes 393224 | tf_op jit(solution)/shard_map/ppermute | solution.py:772
  367.7 6.9 %collective-permute-start.24 = (bf16[4,128,128]{2,1,0:T(8,128)(2,1)S(1)}, bf16[4,128,128]{2,1,0:T(8,128)(2,1)S(1)}, u32[]{:S(2)}, u32[]{:S(2)}) collective-permute-start(bf16[4,128,128]{2,1,0:T(8,128)(2,1)S(1)} %get-tuple-element.165), channel_id=1, source_target_pairs={{0,4},{2,6},{4,0},{6,2},{8,12},{10,14},{12,8},{14,10},{16,20},{18,... | collective-permute-start | bytes 393224 | tf_op jit(solution)/shard_map/ppermute | solution.py:776
  368.3 6.3 %collective-permute-start.25 = (bf16[4,128,128]{2,1,0:T(8,128)(2,1)S(1)}, bf16[4,128,128]{2,1,0:T(8,128)(2,1)S(1)}, u32[]{:S(2)}, u32[]{:S(2)}) collective-permute-start(bf16[4,128,128]{2,1,0:T(8,128)(2,1)S(1)} %get-tuple-element.166), channel_id=1, source_target_pairs={{0,6},{2,4},{4,2},{6,0},{8,14},{10,12},{12,10},{14,8},{16,22},{18,... | collective-permute-start | bytes 393224 | tf_op jit(solution)/shard_map/ppermute | solution.py:1124
  375.2 18.0 %collective-permute-start.26 = (bf16[128,128]{1,0:T(8,128)(2,1)S(1)}, bf16[128,128]{1,0:T(8,128)(2,1)S(1)}, u32[]{:S(2)}, u32[]{:S(2)}) collective-permute-start(bf16[128,128]{1,0:T(8,128)(2,1)S(1)} %get-tuple-element.168), channel_id=1, source_target_pairs={{0,8},{2,10},{4,12},{6,14},{8,16},{10,18},{12,20},{14,22},{16,24},... | collective-permute-start | bytes 98312 | tf_op jit(solution)/shard_map/ppermute | solution.py:781
  377.9 15.3 %collective-permute-start.27 = (bf16[128,128]{1,0:T(8,128)(2,1)S(1)}, bf16[128,128]{1,0:T(8,128)(2,1)S(1)}, u32[]{:S(2)}, u32[]{:S(2)}) collective-permute-start(bf16[128,128]{1,0:T(8,128)(2,1)S(1)} %get-tuple-element.169), channel_id=1, source_target_pairs={{0,16},{2,18},{4,20},{6,22},{8,24},{10,26},{12,28},{14,30},{16,0},... | collective-permute-start | bytes 98312 | tf_op jit(solution)/shard_map/ppermute | solution.py:781
  379.7 13.6 %collective-permute-start.28 = (bf16[128,128]{1,0:T(8,128)(2,1)S(1)}, bf16[128,128]{1,0:T(8,128)(2,1)S(1)}, u32[]{:S(2)}, u32[]{:S(2)}) collective-permute-start(bf16[128,128]{1,0:T(8,128)(2,1)S(1)} %get-tuple-element.170), channel_id=1, source_target_pairs={{0,24},{2,26},{4,28},{6,30},{8,0},{10,2},{12,4},{14,6},{16,8},{18,... | collective-permute-start | bytes 98312 | tf_op jit(solution)/shard_map/ppermute | solution.py:781
  (32 other events, 388.6 us)
Sparse Core Ops, SparseCore 0:
  34.0 155.9 all-gather.2
